TPU v7x, 256 devices: a whole 4x4x8 slice. The times are simulated.
256 devices in a mesh: frame: 32 (over x, z), row: 8 (over y, core).
Axes of the slice: x: 4, y: 4, z: 8, core: 2. Of those that a mesh axis runs over, the one named last changes fastest.
Arguments:
- query_in: bfloat16 [128, 8, 32, 2240], P('frame', 'row'), may hold values from -6 to 6
- key_in: bfloat16 [128, 8, 32, 2240], P('frame', 'row'), may hold values from -24 to 24, as said below
- value_in: bfloat16 [128, 8, 32, 2240], P('frame', 'row'), may hold values from -32 to 32, as said below
- hidden_in: bfloat16 [128, 8, 32, 2240], P('frame', 'row'), may hold values from -16 to 16, as said below
- out_weight: bfloat16 [2240, 2240], replicated, may hold values from -0.125 to 0.125
- norm_gain: float32 [2240], replicated, may hold values from 0.25 to 1.75
- temporal_taps: float32 [3, 2240], replicated, may hold values from -3.5 to 3.5
- block_valid: int32 [32], P('frame'), may hold values from 1 to 4, as said below
Outputs:
- mixed: bfloat16 [128, 8, 32, 2240], P('frame', 'row')
Inputs may be any that keep to these rules, and one draw needn't show every extreme that they name: key_in lies within this range. value_in lies within this range. hidden_in lies within this range. `block_valid`: the first frame block is full.
All inputs are finite; a program needn't handle non-finite values.
Results may differ from a plain program's by a relative error of at most 0.0058.
Values may be sent and summed in bfloat16 or wider, within the bound.
No kernel may reach another device: no remote copies, remote signals or barrier semaphores. Data moves between devices by JAX's collectives and lax.ppermute only.
A program may use at most 128 MiB of HBM per device.

v0:
```python
import functools

import jax
import jax.numpy as jnp
from jax import lax
from jax.experimental import pallas as pl
from jax.experimental.pallas import tpu as pltpu
from jax.sharding import Mesh, PartitionSpec as P


HEADS = 20
DH = 112
LANES = 128
PIECE = 14
GROUP = HEADS // 2
ROWS = 1024
EPS_DEN = 1e-06
EPS_NORM = 1e-06
X, Z, Y, C = 4, 8, 4, 2
CHUNK = 512


def smem():
    return pl.BlockSpec(memory_space=pltpu.SMEM)


def vmem():
    return pl.BlockSpec(memory_space=pltpu.VMEM)


def limit(mib):
    return pltpu.CompilerParams(vmem_limit_bytes=mib << 20)


def cost(micros):
    return pl.CostEstimate(flops=micros * 1_000_000_000, bytes_accessed=1 << 20, transcendentals=0)


def lane_of(shape):
    return lax.broadcasted_iota(jnp.int32, shape, 1)


def place_of(h):
    return (h * DH) // LANES, (h * DH) % LANES


def free_of(h):
    return ((h + 1) * DH) % LANES


def turn_kernel(valid_ref, key_ref, out_ref):
    tokens, features = key_ref.shape
    row = lax.broadcasted_iota(jnp.int32, (tokens, LANES), 0)
    live = row < valid_ref[0] * 32
    for start in range(0, features, LANES):
        width = min(LANES, features - start)
        keys = jnp.maximum(key_ref[:, start : start + width], 0)
        keys = jnp.where(live[:, :width], keys, jnp.zeros_like(keys))
        out_ref[start : start + width, :] = keys.T


def turn(valid, key):
    tokens, features = key.shape
    return pl.pallas_call(
        turn_kernel,
        out_shape=jax.ShapeDtypeStruct((features, tokens), jnp.bfloat16),
        in_specs=[smem(), vmem()],
        out_specs=vmem(),
        compiler_params=limit(8),
        cost_estimate=cost(4),
        name="turn",
    )(valid, key)


def group_states(group, turned, value_ref, out_ref):
    tokens, features = value_ref.shape
    lane = lane_of((tokens, LANES))
    one = jnp.ones((tokens, LANES), jnp.bfloat16)
    lanes = lane_of((DH, LANES))

    def values_at(start):
        width = min(LANES, features - start)
        values = value_ref[:, start : start + width]
        if width < LANES:
            values = jnp.concatenate(
                [values, jnp.zeros((tokens, LANES - width), jnp.bfloat16)], axis=1
            )
        return values

    def head(h):
        tile, off = place_of(h)
        keys = turned[h * DH : (h + 1) * DH, :]
        low = values_at(tile * LANES)
        if off == 0:
            low = jnp.where(lane == DH, one, low)
            return jnp.dot(keys, low, preferred_element_type=jnp.float32)
        high = jnp.where(lane == free_of(h), one, values_at((tile + 1) * LANES))
        wide = jnp.dot(
            keys, jnp.concatenate([low, high], axis=1), preferred_element_type=jnp.float32
        )
        return jnp.where(lanes >= off, wide[:, :LANES], wide[:, LANES:])

    end = group * GROUP + GROUP - 1
    last = head(end)
    for p in range(GROUP - 1):
        h = group * GROUP + p
        free = free_of(h)
        state = head(h)
        if p < 8:
            shift = (free + 2 - place_of(end)[1] - PIECE * p) % LANES
            mask = (lanes >= free + 2) & (lanes < free + 16)
        else:
            shift = (free + 1 - free_of(end)) % LANES
            mask = lanes == free + 1
        moved = pltpu.roll(last, shift, axis=1) if shift else last
        state = jnp.where(mask, moved, state)
        out_ref[p * DH : (p + 1) * DH, :] = state.astype(out_ref.dtype)
    rest = ROWS - (GROUP - 1) * DH
    out_ref[(GROUP - 1) * DH :, :] = jnp.zeros((rest, LANES), out_ref.dtype)


def state_kernel(mine, ids_ref, turned, value_ref, out_ref):
    for group in range(2):

        @pl.when(ids_ref[0] == (group if mine else 1 - group))
        def _():
            group_states(group, turned, value_ref, out_ref)


def local_states(ids, turned, value, mine):
    return pl.pallas_call(
        functools.partial(state_kernel, mine),
        out_shape=jax.ShapeDtypeStruct((ROWS, LANES), jnp.float32 if mine else jnp.bfloat16),
        in_specs=[smem(), vmem(), vmem()],
        out_specs=vmem(),
        compiler_params=limit(12),
        cost_estimate=cost(1),
        name="kept_states" if mine else "sent_states",
    )(ids, turned, value)


def prefix_kernel(got_ref, prefix_ref, whole_ref):
    total = jnp.zeros(prefix_ref.shape[1:], jnp.float32)
    for z in range(Z):
        for y in range(Y):
            total = total + got_ref[z * Y + y].astype(jnp.float32)
        prefix_ref[z] = total
    for x in range(X):
        whole_ref[x] = total


def prefixes(got):
    piece = got.shape[1:]
    return pl.pallas_call(
        prefix_kernel,
        out_shape=(
            jax.ShapeDtypeStruct((Z,) + piece, jnp.float32),
            jax.ShapeDtypeStruct((X,) + piece, jnp.float32),
        ),
        in_specs=[vmem()],
        out_specs=(vmem(), vmem()),
        compiler_params=limit(4),
        cost_estimate=cost(8),
        name="prefixes",
    )(got)


def totals_kernel(ids_ref, prefix_ref, whole_ref, out_ref):
    before = jnp.zeros(prefix_ref.shape[1:], jnp.float32)
    for x in range(X):
        before = before + jnp.where(x < ids_ref[1], whole_ref[x], 0.0)
    for z in range(Z):
        total = (prefix_ref[z] + before).astype(jnp.bfloat16)
        for y in range(Y):
            out_ref[z * Y + y] = total


def totals(place, prefix, whole):
    piece = prefix.shape[1:]
    return pl.pallas_call(
        totals_kernel,
        out_shape=jax.ShapeDtypeStruct((Z * Y,) + piece, jnp.bfloat16),
        in_specs=[smem(), vmem(), vmem()],
        out_specs=vmem(),
        compiler_params=limit(4),
        cost_estimate=cost(8),
        name="totals",
    )(place, prefix, whole)


def project(
    ids_ref, valid_ref, own_ref, other_ref, query_ref, hidden_ref, gain_ref, weight, first, attended, residual, normed_ref
):
    count, features = query_ref.shape
    step = count // 2
    own = ids_ref[0]
    lanes = lane_of((DH, LANES))
    zero = jnp.zeros((DH, LANES), jnp.bfloat16)

    def stored(group, p):
        at = slice(p * DH, (p + 1) * DH)
        return jnp.where(own == group, own_ref[at, :], other_ref[at, :])

    def unpack(group):
        packed = [stored(group, p) for p in range(GROUP - 1)]
        end = group * GROUP + GROUP - 1
        off = place_of(end)[1]
        last = jnp.zeros((DH, LANES), jnp.float32)
        for p in range(GROUP - 1):
            free = free_of(group * GROUP + p)
            if p < 8:
                shift = (off + PIECE * p - free - 2) % LANES
                start = (off + PIECE * p) % LANES
                mask = (lanes >= start) & (lanes < start + PIECE)
                if start + PIECE > LANES:
                    mask = mask | (lanes < start + PIECE - LANES)
            else:
                shift = (free_of(end) - free - 1) % LANES
                mask = lanes == free_of(end)
            wide = packed[p].astype(jnp.float32)
            moved = pltpu.roll(wide, shift, axis=1) if shift else wide
            last = jnp.where(mask, moved, last)
        return packed + [last.astype(jnp.bfloat16)]

    def window(h, packed):
        off = place_of(h)[1]
        if off == 0:
            return jnp.where(lanes <= DH, packed, zero)
        low = jnp.where(lanes >= off, packed, zero)
        high = jnp.where(lanes <= off - 16, packed, zero)
        return jnp.concatenate([low, high], axis=1)

    row = lax.broadcasted_iota(jnp.int32, (count, 1), 0)
    live = (row + first * step < valid_ref[0] * step).astype(jnp.float32)
    lane = lane_of((count, LANES))
    carry = None
    for group in range(2):
        unpacked = unpack(group)
        for p in range(GROUP):
            h = group * GROUP + p
            tile, off = place_of(h)
            start = tile * LANES
            stop = min(start + (LANES if off == 0 else 2 * LANES), features)
            wide = window(h, unpacked[p])
            parts = [wide]
            if off:
                parts.insert(0, jnp.zeros((off, wide.shape[1]), jnp.bfloat16))
            rest = stop - start - off - DH
            if rest:
                parts.append(jnp.zeros((rest, wide.shape[1]), jnp.bfloat16))
            matrix = jnp.concatenate(parts, axis=0) if len(parts) > 1 else wide
            query = jnp.maximum(query_ref[:, start:stop], 0)
            got = jnp.dot(query, matrix, preferred_element_type=jnp.float32)
            below = got[:, off + DH : off + DH + 1] + EPS_DEN
            scale = jnp.broadcast_to(live / below, (count, LANES))
            low = got[:, :LANES] * scale
            if off == 0:
                carry = low
                continue
            full = jnp.where(lane >= off, low, carry)
            attended[:, start : start + LANES] = full.astype(jnp.bfloat16)
            carry = got[:, LANES:] * scale
    left = features % LANES
    if left:
        attended[:, features - left :] = carry[:, :left].astype(jnp.bfloat16)

    squares = jnp.zeros((count, LANES), jnp.float32)
    for s in range(0, features, CHUNK):
        w = min(CHUNK, features - s)
        projected = jnp.dot(
            attended[...], weight[:, s : s + w], preferred_element_type=jnp.float32
        )
        rounded = (hidden_ref[:, s : s + w].astype(jnp.float32) + projected).astype(jnp.bfloat16)
        residual[:, s : s + w] = rounded
        wide = rounded.astype(jnp.float32)
        wide = wide * wide
        for a in range(0, w, LANES):
            b = min(LANES, w - a)
            part = wide[:, a : a + b]
            if b < LANES:
                part = jnp.concatenate([part, jnp.zeros((count, LANES - b), jnp.float32)], axis=1)
            squares = squares + part
    mean = jnp.sum(squares, axis=1, keepdims=True) / features
    inverse = jnp.broadcast_to(lax.rsqrt(mean + EPS_NORM), (count, LANES))
    for s in range(0, features, LANES):
        w = min(LANES, features - s)
        here = residual[:, s : s + w].astype(jnp.float32)
        normed = (here * inverse[:, :w] * gain_ref[:, s : s + w]).astype(jnp.bfloat16)
        normed_ref[:, s : s + w] = normed


def tail_kernel(ids_ref, valid_ref, own_ref, other_ref, query_ref, hidden_ref, gain_ref, weight, residual, normed_ref, attended):
    half = query_ref.shape[0] // 2
    project(
        ids_ref, valid_ref, own_ref, other_ref, query_ref.at[half:, :], hidden_ref.at[half:, :],
        gain_ref, weight, 2, attended, residual, normed_ref,
    )


def tail_of(ids, valid, own, other, query, hidden, gain, weight):
    tokens, features = query.shape
    half = jax.ShapeDtypeStruct((tokens // 2, features), jnp.bfloat16)
    return pl.pallas_call(
        tail_kernel,
        out_shape=(half, half),
        in_specs=[smem(), smem()] + [vmem()] * 6,
        out_specs=(vmem(), vmem()),
        scratch_shapes=[pltpu.VMEM(half.shape, jnp.bfloat16)],
        compiler_params=limit(24),
        cost_estimate=cost(3),
        name="tail_of",
    )(ids, valid, own, other, query, hidden, gain, weight)


def head_kernel(
    ids_ref, valid_ref, own_ref, other_ref, query_ref, hidden_ref, gain_ref, weight,
    tail_residual, tail_normed, taps_ref, out_ref, residual, partial_ref, attended, normed_ref
):
    count, features = residual.shape
    step = count // 2
    project(
        ids_ref, valid_ref, own_ref, other_ref, query_ref.at[:count, :], hidden_ref.at[:count, :],
        gain_ref, weight, 0, attended, residual, normed_ref,
    )
    for s in range(0, features, LANES):
        w = min(LANES, features - s)
        taps = [taps_ref[j : j + 1, s : s + w] for j in range(3)]
        frames = [
            ref[t * step : (t + 1) * step, s : s + w].astype(jnp.float32)
            for ref in (normed_ref, tail_normed)
            for t in range(2)
        ]
        partial_ref[:step, s : s + w] = taps[0] * frames[0]
        partial_ref[step:, s : s + w] = taps[0] * frames[1] + taps[1] * frames[0]
        for t in range(2):
            total = taps[0] * frames[t + 2] + taps[1] * frames[t + 1] + taps[2] * frames[t]
            temporal = total.astype(jnp.bfloat16).astype(jnp.float32)
            at = slice(t * step, (t + 1) * step)
            here = tail_residual[at, s : s + w].astype(jnp.float32)
            out_ref[at, s : s + w] = (here + temporal).astype(jnp.bfloat16)


def head_of(ids, valid, own, other, query, hidden, gain, weight, tail_residual, tail_normed, taps):
    tokens, features = query.shape
    half = (tokens // 2, features)
    return pl.pallas_call(
        head_kernel,
        grid=(1,),
        out_shape=(
            jax.ShapeDtypeStruct(query.shape, jnp.bfloat16),
            jax.ShapeDtypeStruct(half, jnp.bfloat16),
            jax.ShapeDtypeStruct(half, jnp.float32),
        ),
        in_specs=[smem(), smem()] + [vmem()] * 9,
        out_specs=(pl.BlockSpec(half, lambda i: (1, 0)), vmem(), vmem()),
        scratch_shapes=[pltpu.VMEM(half, jnp.bfloat16), pltpu.VMEM(half, jnp.bfloat16)],
        compiler_params=limit(24),
        cost_estimate=cost(3),
        name="head_of",
    )(ids, valid, own, other, query, hidden, gain, weight, tail_residual, tail_normed, taps)


def finish_kernel(unused_ref, residual_ref, partial_ref, halo_ref, taps_ref, out_ref):
    count, features = residual_ref.shape
    step = count // 2
    for s in range(0, features, LANES):
        w = min(LANES, features - s)
        taps = [taps_ref[j : j + 1, s : s + w] for j in range(3)]
        oldest = halo_ref[:step, s : s + w].astype(jnp.float32)
        older = halo_ref[step:, s : s + w].astype(jnp.float32)
        totals = [
            partial_ref[:step, s : s + w] + taps[1] * older + taps[2] * oldest,
            partial_ref[step:, s : s + w] + taps[2] * older,
        ]
        for t, total in enumerate(totals):
            temporal = total.astype(jnp.bfloat16).astype(jnp.float32)
            at = slice(t * step, (t + 1) * step)
            here = residual_ref[at, s : s + w].astype(jnp.float32)
            out_ref[at, s : s + w] = (here + temporal).astype(jnp.bfloat16)


def finish(out, residual, partial, halo, taps):
    return pl.pallas_call(
        finish_kernel,
        grid=(1,),
        out_shape=jax.ShapeDtypeStruct(out.shape, out.dtype),
        in_specs=[pl.BlockSpec(memory_space=pl.ANY)] + [vmem()] * 4,
        out_specs=pl.BlockSpec(residual.shape, lambda i: (0, 0)),
        input_output_aliases={0: 0},
        compiler_params=limit(8),
        cost_estimate=cost(1),
        name="finish",
    )(out, residual, partial, halo, taps)


def body(query_in, key_in, value_in, hidden_in, out_weight, norm_gain, temporal_taps, block_valid):
    frames, rows_dev, width_cols, features = query_in.shape
    tokens = frames * rows_dev * width_cols
    ids = jnp.stack([lax.axis_index("core"), lax.axis_index("x")]).astype(jnp.int32)
    query = query_in.reshape(tokens, features)
    hidden = hidden_in.reshape(tokens, features)
    swap = [(0, 1), (1, 0)]
    keys = turn(block_valid, key_in.reshape(tokens, features))
    value = value_in.reshape(tokens, features)
    send = local_states(ids, keys, value, False)
    fetched = lax.ppermute(send, "core", swap)
    keep = local_states(ids, keys, value, True)
    mine = (keep + fetched.astype(jnp.float32)).astype(jnp.bfloat16)
    piece = ROWS // (Z * Y)
    got = lax.all_to_all(mine, ("z", "y"), 0, 0, tiled=True).reshape(Z * Y, piece, LANES)
    prefix, whole = prefixes(got)
    wholes = lax.all_to_all(whole, "x", 0, 0, tiled=True)
    own = lax.all_to_all(totals(ids, prefix, wholes), ("z", "y"), 0, 0, tiled=True)
    own = own.reshape(ROWS, LANES)
    other = lax.ppermute(own, "core", swap)
    gain = norm_gain.reshape(1, features)
    shared = (ids, block_valid, own, other, query, hidden, gain, out_weight)
    tail_residual, tail_normed = tail_of(*shared)
    halo = lax.ppermute(tail_normed, ("x", "z"), [(i, i + 1) for i in range(X * Z - 1)])
    out, residual, partial = head_of(*shared, tail_residual, tail_normed, temporal_taps)
    mixed = finish(out, residual, partial, halo, temporal_taps)
    return mixed.reshape(query_in.shape)


def solution(mesh):
    fine = Mesh(mesh.devices.reshape(X, Z, Y, C), ("x", "z", "y", "core"))
    token = P(("x", "z"), ("y", "core"), None, None)
    placed = (token, token, token, token, P(), P(), P(), P(("x", "z")))

    return jax.shard_map(body, mesh=fine, in_specs=placed, out_specs=token, check_vma=False)
```

profile of v0, /device:TPU:2, one launch (start us, length us, event | category | flops | bytes accessed | tf_op | source)
XLA Modules:
  0.0 73.5 jit_solution(11802346504607895744)
XLA Ops:
  0.7 0.1 pad_add_fusion.ids_ref
  0.7 0.0 copy-start.3
  0.7 1.1 %copy-done.3 = bf16[4,1,32,2240]{3,2,1,0:T(8,128)(2,1)S(1)} copy-done((bf16[4,1,32,2240]{3,2,1,0:T(8,128)(2,1)S(1)}, bf16[4,1,32,2240]{3,2,1,0:T(8,128)(2,1)}, u32[]{:S(2)}) %copy-start.3) | copy-done | bytes 573464
  1.8 0.0 copy-start.4
  1.8 0.2 turn.1.turned
  2.0 0.9 %copy-done.4 = bf16[4,1,32,2240]{3,2,1,0:T(8,128)(2,1)S(1)} copy-done((bf16[4,1,32,2240]{3,2,1,0:T(8,128)(2,1)S(1)}, bf16[4,1,32,2240]{3,2,1,0:T(8,128)(2,1)}, u32[]{:S(2)}) %copy-start.4) | copy-done | bytes 573464
  2.9 0.9 %sent_states.1 = bf16[1024,128]{1,0:T(8,128)(2,1)S(1)} custom-call(s32[2]{0:T(128)S(1)} %pad_add_fusion.ids_ref, bf16[2240,128]{1,0:T(8,128)(2,1)S(1)} %turn.1.turned, bf16[128,2240]{1,0:T(8,128)(2,1)S(1)} %bitcast.21), custom_call_target="tpu_custom_call" | custom-call | flops 1000000000 | bytes 1048576 | tf_op jit(solution)/shard_map/sent_states/pallas_call | solution.py:131
  3.7 0.1 collective-permute-start
  3.8 0.9 %kept_states.1 = f32[1024,128]{1,0:T(8,128)S(1)} custom-call(s32[2]{0:T(128)S(1)} %pad_add_fusion.ids_ref, bf16[2240,128]{1,0:T(8,128)(2,1)S(1)} %turn.1.turned, bf16[128,2240]{1,0:T(8,128)(2,1)S(1)} %bitcast.22), custom_call_target="tpu_custom_call" | custom-call | flops 1000000000 | bytes 1048576 | tf_op jit(solution)/shard_map/kept_states/pallas_call | solution.py:131
  4.7 0.6 collective-permute-done
  5.3 0.1 add_convert_fusion
  5.4 24.5 %all_to_all.19.got_ref = bf16[32,32,128]{2,1,0:T(8,128)(2,1)S(1)} all-to-all(bf16[32,32,128]{2,1,0:T(8,128)(2,1)S(1)} %bitcast.23), channel_id=1, replica_groups=mesh['x'=4,'z'=8,'y'=4,'core'=2] {'z','y'}, dimensions={0} | all-to-all | bytes 524288 | tf_op jit(solution)/shard_map/all_to_all | solution.py:410
  30.0 0.0 slice-start
  30.0 0.0 slice-start.1
  30.0 9.1 %all_to_all.20.whole_ref = f32[4,32,128]{2,1,0:T(8,128)S(1)} all-to-all(f32[4,32,128]{2,1,0:T(8,128)S(1)} %get-tuple-element.13), channel_id=1, replica_groups=mesh['x'=4,'z'=8,'y'=4,'core'=2] {'x'}, dimensions={0} | all-to-all | bytes 131072 | tf_op jit(solution)/shard_map/all_to_all | solution.py:412
  39.1 0.6 totals.1
  39.6 0.0 copy-start.2
  39.7 15.6 %all_to_all.21 = bf16[32,32,128]{2,1,0:T(8,128)(2,1)S(1)} all-to-all(bf16[32,32,128]{2,1,0:T(8,128)(2,1)S(1)} %totals.1), channel_id=1, replica_groups=mesh['x'=4,'z'=8,'y'=4,'core'=2] {'z','y'}, dimensions={0} | all-to-all | bytes 524288 | tf_op jit(solution)/shard_map/all_to_all | solution.py:413
  55.2 0.0 collective-permute-start.1
  55.3 0.0 copy-done.5
  55.3 1.5 %collective-permute-done.1.other_ref = bf16[1024,128]{1,0:T(8,128)(2,1)S(1)} collective-permute-done((bf16[1024,128]{1,0:T(8,128)(2,1)S(1)}, bf16[1024,128]{1,0:T(8,128)(2,1)S(1)}, u32[]{:S(2)}, u32[]{:S(2)}) %collective-permute-start.1) | collective-permute-done | bytes 262176 | tf_op jit(solution)/shard_map/ppermute | solution.py:415
  56.8 0.0 slice-done
  56.8 0.0 slice-done.1
  56.8 0.0 slice-done.2
  56.8 0.0 copy-done
  56.8 0.0 copy-done.1
  56.8 2.8 %tail_of.1 = (bf16[64,2240]{1,0:T(8,128)(2,1)S(1)}, bf16[64,2240]{1,0:T(8,128)(2,1)S(1)}) custom-call(s32[2]{0:T(128)S(1)} %pad_add_fusion.ids_ref, s32[1]{0:T(128)S(6)} %copy.12.valid_ref, bf16[1024,128]{1,0:T(8,128)(2,1)S(1)} %bitcast.18, bf16[1024,128]{1,0:T(8,128)(2,1)S(1)} %collective-permute-done.1.other_ref, bf16[128,2240]{1,0:T(8,128)(2,1)S(1)} %bitcast.13, ...), custom_call_target="tpu_custom_call" | custom-call | flops 3000000000 | bytes 1048576 | tf_op jit(solution)/shard_map/tail_of/pallas_call | solution.py:303
  59.6 2.7 %collective-permute-start.2 = (bf16[64,2240]{1,0:T(8,128)(2,1)S(1)}, bf16[64,2240]{1,0:T(8,128)(2,1)S(1)}, u32[]{:S(2)}, u32[]{:S(2)}) collective-permute-start(bf16[64,2240]{1,0:T(8,128)(2,1)S(1)} %get-tuple-element.15.tail_normed), channel_id=1, source_target_pairs={{0,8},{8,16},{16,24},{24,32},{32,40},{40,48},{48,56},{56,64},{64,7... | collective-permute-start | bytes 860168 | tf_op jit(solution)/shard_map/ppermute | solution.py:419
  62.3 0.0 copy-done.2
  62.3 3.8 %head_of.1 = (bf16[128,2240]{1,0:T(8,128)(2,1)}, bf16[64,2240]{1,0:T(8,128)(2,1)S(1)}, f32[64,2240]{1,0:T(8,128)S(1)}) custom-call(s32[2]{0:T(128)S(1)} %pad_add_fusion.ids_ref, s32[1]{0:T(128)S(6)} %copy.12.valid_ref, bf16[1024,128]{1,0:T(8,128)(2,1)S(1)} %bitcast.19, bf16[1024,128]{1,0:T(8,128)(2,1)S(1)} %collective-permute-done.1.other_ref, ...), custom_call_target="tpu_custom_call" | custom-call | flops 3000000000 | bytes 1048576 | tf_op jit(solution)/shard_map/head_of/pallas_call | solution.py:346
  66.1 6.5 %collective-permute-done.2.halo_ref = bf16[64,2240]{1,0:T(8,128)(2,1)S(1)} collective-permute-done((bf16[64,2240]{1,0:T(8,128)(2,1)S(1)}, bf16[64,2240]{1,0:T(8,128)(2,1)S(1)}, u32[]{:S(2)}, u32[]{:S(2)}) %collective-permute-start.2) | collective-permute-done | bytes 286752 | tf_op jit(solution)/shard_map/ppermute | solution.py:419
  72.7 0.9 %finish.1 = bf16[128,2240]{1,0:T(8,128)(2,1)} custom-call(bf16[128,2240]{1,0:T(8,128)(2,1)} %get-tuple-element.16.unused_ref, bf16[64,2240]{1,0:T(8,128)(2,1)S(1)} %get-tuple-element.17.residual_ref, f32[64,2240]{1,0:T(8,128)S(1)} %get-tuple-element.18.partial_ref, ...), custom_call_target="tpu_custom_call", output_to_operand_aliasing={{}: (0, {})} | custom-call | flops 1000000000 | bytes 1048576 | tf_op jit(solution)/shard_map/finish/pallas_call | solution.py:383
  (7 shorter events, 0.1 us)
Async XLA Ops:
  0.7 1.1 %copy-start.3 = (bf16[4,1,32,2240]{3,2,1,0:T(8,128)(2,1)S(1)}, bf16[4,1,32,2240]{3,2,1,0:T(8,128)(2,1)}, u32[]{:S(2)}) copy-start(bf16[4,1,32,2240]{3,2,1,0:T(8,128)(2,1)} %param.9) | copy-start | bytes 1720324
  1.8 1.1 %copy-start.4 = (bf16[4,1,32,2240]{3,2,1,0:T(8,128)(2,1)S(1)}, bf16[4,1,32,2240]{3,2,1,0:T(8,128)(2,1)}, u32[]{:S(2)}) copy-start(bf16[4,1,32,2240]{3,2,1,0:T(8,128)(2,1)} %param.10) | copy-start | bytes 1720324
  3.7 1.6 %collective-permute-start = (bf16[1024,128]{1,0:T(8,128)(2,1)S(1)}, bf16[1024,128]{1,0:T(8,128)(2,1)S(1)}, u32[]{:S(2)}, u32[]{:S(2)}) collective-permute-start(bf16[1024,128]{1,0:T(8,128)(2,1)S(1)} %sent_states.1), channel_id=1, source_target_pairs={{0,1},{1,0},{2,3},{3,2},{4,5},{5,4},{6,7},{7,6},{8,9},{9,8},{10,11... | collective-permute-start | bytes 786440 | tf_op jit(solution)/shard_map/ppermute | solution.py:406
  30.0 26.8 %slice-start = ((s8[10321920]{0:T(1024)(128)(4,1)}), s8[4194304]{0:T(1024)(128)(4,1)S(1)}, s32[]{:S(2)}) async-start(s8[10321920]{0:T(1024)(128)(4,1)} %bitcast.11), calls=%async_computation.3 | async-start | bytes 8388608
  30.0 26.8 %slice-start.1 = ((s8[10321920]{0:T(1024)(128)(4,1)}), s8[4194304]{0:T(1024)(128)(4,1)S(1)}, s32[]{:S(2)}) async-start(s8[10321920]{0:T(1024)(128)(4,1)} %bitcast.11), calls=%async_computation.4 | async-start | bytes 8388608
  39.1 16.2 %copy-start.5 = (f32[2240]{0:T(1024)S(1)}, f32[2240]{0:T(1024)}, u32[]{:S(2)}) copy-start(f32[2240]{0:T(1024)} %param.13) | copy-start | bytes 26884
  39.1 17.7 %slice-start.2 = ((s8[10321920]{0:T(1024)(128)(4,1)}), s8[1933312]{0:T(1024)(128)(4,1)S(1)}, s32[]{:S(2)}) async-start(s8[10321920]{0:T(1024)(128)(4,1)} %bitcast.11), calls=%async_computation.5 | async-start | bytes 3866624
  39.1 17.7 %copy-start = (bf16[4,1,32,2240]{3,2,1,0:T(8,128)(2,1)S(1)}, bf16[4,1,32,2240]{3,2,1,0:T(8,128)(2,1)}, u32[]{:S(2)}) copy-start(bf16[4,1,32,2240]{3,2,1,0:T(8,128)(2,1)} %param.8) | copy-start | bytes 1720324
  39.1 17.7 %copy-start.1 = (bf16[4,1,32,2240]{3,2,1,0:T(8,128)(2,1)S(1)}, bf16[4,1,32,2240]{3,2,1,0:T(8,128)(2,1)}, u32[]{:S(2)}) copy-start(bf16[4,1,32,2240]{3,2,1,0:T(8,128)(2,1)} %param.11) | copy-start | bytes 1720324
  39.6 22.7 %copy-start.2 = (f32[3,2240]{1,0:T(4,128)S(1)}, f32[3,2240]{1,0:T(4,128)}, u32[]{:S(2)}) copy-start(f32[3,2240]{1,0:T(4,128)} %taps_ref.3) | copy-start | bytes 80644
  55.2 1.5 %collective-permute-start.1 = (bf16[1024,128]{1,0:T(8,128)(2,1)S(1)}, bf16[1024,128]{1,0:T(8,128)(2,1)S(1)}, u32[]{:S(2)}, u32[]{:S(2)}) collective-permute-start(bf16[1024,128]{1,0:T(8,128)(2,1)S(1)} %bitcast.17), channel_id=1, source_target_pairs={{0,1},{1,0},{2,3},{3,2},{4,5},{5,4},{6,7},{7,6},{8,9},{9,8},{10,11... | collective-permute-start | bytes 786440 | tf_op jit(solution)/shard_map/ppermute | solution.py:415
  59.6 13.0 %collective-permute-start.2 = (bf16[64,2240]{1,0:T(8,128)(2,1)S(1)}, bf16[64,2240]{1,0:T(8,128)(2,1)S(1)}, u32[]{:S(2)}, u32[]{:S(2)}) collective-permute-start(bf16[64,2240]{1,0:T(8,128)(2,1)S(1)} %get-tuple-element.15.tail_normed), channel_id=1, source_target_pairs={{0,8},{8,16},{16,24},{24,32},{32,40},{40,48},{48,56},{56,64},{64,7... | collective-permute-start | bytes 860168 | tf_op jit(solution)/shard_map/ppermute | solution.py:419
where the time goes:
time: 73.8 us; the launch traced here: 73.5 us
  blocking collectives  49.2 us (67%)
  Pallas kernels  10.1 us (14%)
  waiting for transfers between devices  8.63 us (12%)
  starting transfers between devices  2.77 us (4%)
  local copies, waits for them, and re-layouts  1.95 us (3%)
  between operations  0.77 us (1%)
    all_to_all x1, blocking collectives, body(): lax.all_to_all(mine, ('z', 'y'), 0, 0, tiled=True)  24.5 us
    all_to_all x1, blocking collectives, body(): lax.all_to_all(totals(ids, prefix, wholes), ('z', 'y'), 0, 0, tiled=True)  15.6 us
    all_to_all x1, blocking collectives, body(): wholes = lax.all_to_all(whole, 'x', 0, 0, tiled=True)  9.06 us
    ppermute x1, waiting for transfers between devices, body(): lax.ppermute(tail_normed, ('x', 'z'), [(i, i + 1) for i in range(X * Z -...  6.51 us
    pallas_call x1, Pallas kernels, head_of(): pl.pallas_call(head_kernel, grid=(1,), out_shape=(jax.ShapeDtypeStruct(qu...  3.84 us
    pallas_call x1, Pallas kernels, tail_of(): pl.pallas_call(tail_kernel, out_shape=(half, half), in_specs=[smem(), sme...  2.79 us
    ppermute x1, starting transfers between devices, body(): lax.ppermute(tail_normed, ('x', 'z'), [(i, i + 1) for i in range(X * Z -...  2.67 us
    unnamed x18, local copies, waits for them, and re-layouts  1.94 us
  transfers between devices with their start and end apart: 3, of which 3 were waited for; matrix products, arithmetic and copies ran while one was open for 0% of the time, Pallas kernels for 6%

commit v1 on v0

--- a/solution.py
+++ b/solution.py
@@ -46,30 +46,6 @@
 
 def free_of(h):
     return ((h + 1) * DH) % LANES
-
-
-def turn_kernel(valid_ref, key_ref, out_ref):
-    tokens, features = key_ref.shape
-    row = lax.broadcasted_iota(jnp.int32, (tokens, LANES), 0)
-    live = row < valid_ref[0] * 32
-    for start in range(0, features, LANES):
-        width = min(LANES, features - start)
-        keys = jnp.maximum(key_ref[:, start : start + width], 0)
-        keys = jnp.where(live[:, :width], keys, jnp.zeros_like(keys))
-        out_ref[start : start + width, :] = keys.T
-
-
-def turn(valid, key):
-    tokens, features = key.shape
-    return pl.pallas_call(
-        turn_kernel,
-        out_shape=jax.ShapeDtypeStruct((features, tokens), jnp.bfloat16),
-        in_specs=[smem(), vmem()],
-        out_specs=vmem(),
-        compiler_params=limit(8),
-        cost_estimate=cost(4),
-        name="turn",
-    )(valid, key)
 
 
 def group_states(group, turned, value_ref, out_ref):
@@ -119,24 +95,65 @@
     out_ref[(GROUP - 1) * DH :, :] = jnp.zeros((rest, LANES), out_ref.dtype)
 
 
-def state_kernel(mine, ids_ref, turned, value_ref, out_ref):
+def live_kernel(valid_ref, out_ref):
+    tokens = out_ref.shape[0]
+    row = lax.broadcasted_iota(jnp.int32, out_ref.shape, 0)
+    live = row < valid_ref[0] * (tokens // 4)
+    out_ref[...] = jnp.where(live, 1.0, 0.0).astype(jnp.bfloat16)
+
+
+def live_of(valid, tokens):
+    return pl.pallas_call(
+        live_kernel,
+        out_shape=jax.ShapeDtypeStruct((tokens, LANES), jnp.bfloat16),
+        in_specs=[smem()],
+        out_specs=vmem(),
+        compiler_params=limit(2),
+        cost_estimate=cost(8),
+        name="live_of",
+    )(valid)
+
+
+def turn_kernel(live_ref, key_ref, out_ref):
+    _, features = key_ref.shape
+    live = live_ref[...]
+    for start in range(0, features, LANES):
+        width = min(LANES, features - start)
+        keys = jnp.maximum(key_ref[:, start : start + width], 0) * live[:, :width]
+        out_ref[start : start + width, :] = keys.T
+
+
+def turn(live, key):
+    tokens, features = key.shape
+    return pl.pallas_call(
+        turn_kernel,
+        out_shape=jax.ShapeDtypeStruct((features, tokens), jnp.bfloat16),
+        in_specs=[vmem(), vmem()],
+        out_specs=vmem(),
+        compiler_params=limit(8),
+        name="turn",
+    )(live, key)
+
+
+def state_kernel(mine, turned, value_ref, out_ref):
+    core = lax.axis_index("core")
     for group in range(2):
 
-        @pl.when(ids_ref[0] == (group if mine else 1 - group))
+        @pl.when(core == (group if mine else 1 - group))
         def _():
             group_states(group, turned, value_ref, out_ref)
 
 
-def local_states(ids, turned, value, mine):
+def local_states(turned, value, mine):
     return pl.pallas_call(
         functools.partial(state_kernel, mine),
         out_shape=jax.ShapeDtypeStruct((ROWS, LANES), jnp.float32 if mine else jnp.bfloat16),
-        in_specs=[smem(), vmem(), vmem()],
+        in_specs=[vmem(), vmem()],
         out_specs=vmem(),
-        compiler_params=limit(12),
+        compiler_params=limit(8),
         cost_estimate=cost(1),
         name="kept_states" if mine else "sent_states",
-    )(ids, turned, value)
+    )(turned, value)
 
 
 def prefix_kernel(got_ref, prefix_ref, whole_ref):
@@ -165,35 +182,36 @@
     )(got)
 
 
-def totals_kernel(ids_ref, prefix_ref, whole_ref, out_ref):
+def totals_kernel(prefix_ref, whole_ref, out_ref):
+    place = lax.axis_index("x")
     before = jnp.zeros(prefix_ref.shape[1:], jnp.float32)
     for x in range(X):
-        before = before + jnp.where(x < ids_ref[1], whole_ref[x], 0.0)
+        before = before + jnp.where(x < place, whole_ref[x], 0.0)
     for z in range(Z):
         total = (prefix_ref[z] + before).astype(jnp.bfloat16)
         for y in range(Y):
             out_ref[z * Y + y] = total
 
 
-def totals(place, prefix, whole):
+def totals(prefix, whole):
     piece = prefix.shape[1:]
     return pl.pallas_call(
         totals_kernel,
         out_shape=jax.ShapeDtypeStruct((Z * Y,) + piece, jnp.bfloat16),
-        in_specs=[smem(), vmem(), vmem()],
+        in_specs=[vmem(), vmem()],
         out_specs=vmem(),
         compiler_params=limit(4),
         cost_estimate=cost(8),
         name="totals",
-    )(place, prefix, whole)
+    )(prefix, whole)
 
 
 def project(
-    ids_ref, valid_ref, own_ref, other_ref, query_ref, hidden_ref, gain_ref, weight, first, attended, residual, normed_ref
+    valid_ref, own_ref, other_ref, query_ref, hidden_ref, gain_ref, weight, first, attended, residual, normed_ref
 ):
     count, features = query_ref.shape
     step = count // 2
-    own = ids_ref[0]
+    own = lax.axis_index("core")
     lanes = lane_of((DH, LANES))
     zero = jnp.zeros((DH, LANES), jnp.bfloat16)
 
@@ -289,37 +307,37 @@
         normed_ref[:, s : s + w] = normed
 
 
-def tail_kernel(ids_ref, valid_ref, own_ref, other_ref, query_ref, hidden_ref, gain_ref, weight, residual, normed_ref, attended):
+def tail_kernel(valid_ref, own_ref, other_ref, query_ref, hidden_ref, gain_ref, weight, residual, normed_ref, attended):
     half = query_ref.shape[0] // 2
     project(
-        ids_ref, valid_ref, own_ref, other_ref, query_ref.at[half:, :], hidden_ref.at[half:, :],
+        valid_ref, own_ref, other_ref, query_ref.at[half:, :], hidden_ref.at[half:, :],
         gain_ref, weight, 2, attended, residual, normed_ref,
     )
 
 
-def tail_of(ids, valid, own, other, query, hidden, gain, weight):
+def tail_of(valid, own, other, query, hidden, gain, weight):
     tokens, features = query.shape
     half = jax.ShapeDtypeStruct((tokens // 2, features), jnp.bfloat16)
     return pl.pallas_call(
         tail_kernel,
         out_shape=(half, half),
-        in_specs=[smem(), smem()] + [vmem()] * 6,
+        in_specs=[smem()] + [vmem()] * 6,
         out_specs=(vmem(), vmem()),
         scratch_shapes=[pltpu.VMEM(half.shape, jnp.bfloat16)],
         compiler_params=limit(24),
         cost_estimate=cost(3),
         name="tail_of",
-    )(ids, valid, own, other, query, hidden, gain, weight)
+    )(valid, own, other, query, hidden, gain, weight)
 
 
 def head_kernel(
-    ids_ref, valid_ref, own_ref, other_ref, query_ref, hidden_ref, gain_ref, weight,
+    valid_ref, own_ref, other_ref, query_ref, hidden_ref, gain_ref, weight,
     tail_residual, tail_normed, taps_ref, out_ref, residual, partial_ref, attended, normed_ref
 ):
     count, features = residual.shape
     step = count // 2
     project(
-        ids_ref, valid_ref, own_ref, other_ref, query_ref.at[:count, :], hidden_ref.at[:count, :],
+        valid_ref, own_ref, other_ref, query_ref.at[:count, :], hidden_ref.at[:count, :],
         gain_ref, weight, 0, attended, residual, normed_ref,
     )
     for s in range(0, features, LANES):
@@ -340,7 +358,7 @@
             out_ref[at, s : s + w] = (here + temporal).astype(jnp.bfloat16)
 
 
-def head_of(ids, valid, own, other, query, hidden, gain, weight, tail_residual, tail_normed, taps):
+def head_of(valid, own, other, query, hidden, gain, weight, tail_residual, tail_normed, taps):
     tokens, features = query.shape
     half = (tokens // 2, features)
     return pl.pallas_call(
@@ -351,13 +369,13 @@
             jax.ShapeDtypeStruct(half, jnp.bfloat16),
             jax.ShapeDtypeStruct(half, jnp.float32),
         ),
-        in_specs=[smem(), smem()] + [vmem()] * 9,
+        in_specs=[smem()] + [vmem()] * 9,
         out_specs=(pl.BlockSpec(half, lambda i: (1, 0)), vmem(), vmem()),
         scratch_shapes=[pltpu.VMEM(half, jnp.bfloat16), pltpu.VMEM(half, jnp.bfloat16)],
         compiler_params=limit(24),
         cost_estimate=cost(3),
         name="head_of",
-    )(ids, valid, own, other, query, hidden, gain, weight, tail_residual, tail_normed, taps)
+    )(valid, own, other, query, hidden, gain, weight, tail_residual, tail_normed, taps)
 
 
 def finish_kernel(unused_ref, residual_ref, partial_ref, halo_ref, taps_ref, out_ref):
@@ -396,25 +414,24 @@
 def body(query_in, key_in, value_in, hidden_in, out_weight, norm_gain, temporal_taps, block_valid):
     frames, rows_dev, width_cols, features = query_in.shape
     tokens = frames * rows_dev * width_cols
-    ids = jnp.stack([lax.axis_index("core"), lax.axis_index("x")]).astype(jnp.int32)
     query = query_in.reshape(tokens, features)
     hidden = hidden_in.reshape(tokens, features)
     swap = [(0, 1), (1, 0)]
-    keys = turn(block_valid, key_in.reshape(tokens, features))
     value = value_in.reshape(tokens, features)
-    send = local_states(ids, keys, value, False)
+    turned = turn(live_of(block_valid, tokens), key_in.reshape(tokens, features))
+    send = local_states(turned, value, False)
     fetched = lax.ppermute(send, "core", swap)
-    keep = local_states(ids, keys, value, True)
+    keep = local_states(turned, value, True)
     mine = (keep + fetched.astype(jnp.float32)).astype(jnp.bfloat16)
     piece = ROWS // (Z * Y)
     got = lax.all_to_all(mine, ("z", "y"), 0, 0, tiled=True).reshape(Z * Y, piece, LANES)
     prefix, whole = prefixes(got)
     wholes = lax.all_to_all(whole, "x", 0, 0, tiled=True)
-    own = lax.all_to_all(totals(ids, prefix, wholes), ("z", "y"), 0, 0, tiled=True)
+    own = lax.all_to_all(totals(prefix, wholes), ("z", "y"), 0, 0, tiled=True)
     own = own.reshape(ROWS, LANES)
     other = lax.ppermute(own, "core", swap)
     gain = norm_gain.reshape(1, features)
-    shared = (ids, block_valid, own, other, query, hidden, gain, out_weight)
+    shared = (block_valid, own, other, query, hidden, gain, out_weight)
     tail_residual, tail_normed = tail_of(*shared)
     halo = lax.ppermute(tail_normed, ("x", "z"), [(i, i + 1) for i in range(X * Z - 1)])
     out, residual, partial = head_of(*shared, tail_residual, tail_normed, temporal_taps)

time: 73.8 us -> 71.4 us (0.967)
  Pallas kernels: 10.1 us -> 7.42 us
  waiting for transfers between devices: 8.63 us -> 9.74 us
  local copies, waits for them, and re-layouts: 1.95 us -> 1.06 us
    pallas_call x2, Pallas kernels: 1.77 us -> 0.69 us  [local_states(): pl.pallas_call(functools.partial(state_kernel, mine), out_shape=jax.Shape...]
    unnamed x18, local copies, waits for them, and re-layouts: 1.94 us -> 1.06 us
    pallas_call x1 -> x2, Pallas kernels: 2.79 us -> 2.29 us  [the longest x1 2.27 us: tail_of(): pl.pallas_call(tail_kernel, out_shape=(half, half), in_specs=[smem()] + [...]
  transfers between devices with their start and end apart: 3 -> 3, of which waited for: 3 -> 3; matrix products, arithmetic and copies ran while one was open for 0% -> 0% of each run, Pallas kernels for 6% -> 5%
where the time goes in v1:
time: 71.4 us; the launch traced here: 71.2 us
  blocking collectives  49.3 us (69%)
  waiting for transfers between devices  9.74 us (14%)
  Pallas kernels  7.42 us (10%)
  starting transfers between devices  2.77 us (4%)
  local copies, waits for them, and re-layouts  1.06 us (1%)
  between operations  0.8 us (1%)
    all_to_all x1, blocking collectives, body(): lax.all_to_all(mine, ('z', 'y'), 0, 0, tiled=True)  24.5 us
    all_to_all x1, blocking collectives, body(): own = lax.all_to_all(totals(prefix, wholes), ('z', 'y'), 0, 0, tiled=True)  15.7 us
    all_to_all x1, blocking collectives, body(): wholes = lax.all_to_all(whole, 'x', 0, 0, tiled=True)  9.06 us
    ppermute x1, waiting for transfers between devices, body(): lax.ppermute(tail_normed, ('x', 'z'), [(i, i + 1) for i in range(X * Z -...  7.08 us
    pallas_call x1, Pallas kernels, head_of(): pl.pallas_call(head_kernel, grid=(1,), out_shape=(jax.ShapeDtypeStruct(qu...  3.27 us
    ppermute x1, starting transfers between devices, body(): lax.ppermute(tail_normed, ('x', 'z'), [(i, i + 1) for i in range(X * Z -...  2.67 us
    pallas_call x1, Pallas kernels, tail_of(): pl.pallas_call(tail_kernel, out_shape=(half, half), in_specs=[smem()] + [...  2.27 us
    ppermute x1, waiting for transfers between devices, body(): other = lax.ppermute(own, 'core', swap)  1.52 us
  transfers between devices with their start and end apart: 3, of which 3 were waited for; matrix products, arithmetic and copies ran while one was open for 0% of the time, Pallas kernels for 5%

profile of v1, /device:TPU:2, one launch (start us, length us, event | category | flops | bytes accessed | tf_op | source)
XLA Modules:
  0.0 71.2 jit_solution(8284936461038930019)
XLA Ops:
  0.7 0.0 copy-start.2
  0.7 0.0 copy-start.4
  0.7 1.0 %copy-done.2 = bf16[4,1,32,2240]{3,2,1,0:T(8,128)(2,1)S(1)} copy-done((bf16[4,1,32,2240]{3,2,1,0:T(8,128)(2,1)S(1)}, bf16[4,1,32,2240]{3,2,1,0:T(8,128)(2,1)}, u32[]{:S(2)}) %copy-start.2) | copy-done | bytes 573464
  1.7 0.2 turn.1.turned
  1.9 0.0 copy-done.4
  1.9 0.3 sent_states.1
  2.3 0.1 collective-permute-start
  2.4 0.4 kept_states.1
  2.7 1.1 %collective-permute-done = bf16[1024,128]{1,0:T(8,128)(2,1)S(1)} collective-permute-done((bf16[1024,128]{1,0:T(8,128)(2,1)S(1)}, bf16[1024,128]{1,0:T(8,128)(2,1)S(1)}, u32[]{:S(2)}, u32[]{:S(2)}) %collective-permute-start) | collective-permute-done | bytes 262176 | tf_op jit(solution)/shard_map/ppermute | solution.py:423
  3.9 0.1 add_convert_fusion
  3.9 24.5 %all_to_all.19.got_ref = bf16[32,32,128]{2,1,0:T(8,128)(2,1)S(1)} all-to-all(bf16[32,32,128]{2,1,0:T(8,128)(2,1)S(1)} %bitcast.21), channel_id=1, replica_groups=mesh['x'=4,'z'=8,'y'=4,'core'=2] {'z','y'}, dimensions={0} | all-to-all | bytes 524288 | tf_op jit(solution)/shard_map/all_to_all | solution.py:427
  28.5 0.0 slice-start
  28.5 9.1 %all_to_all.20.whole_ref = f32[4,32,128]{2,1,0:T(8,128)S(1)} all-to-all(f32[4,32,128]{2,1,0:T(8,128)S(1)} %get-tuple-element.13), channel_id=1, replica_groups=mesh['x'=4,'z'=8,'y'=4,'core'=2] {'x'}, dimensions={0} | all-to-all | bytes 131072 | tf_op jit(solution)/shard_map/all_to_all | solution.py:429
  37.6 0.0 copy-start.5
  37.6 0.0 slice-start.2
  37.6 0.0 copy-start
  37.6 0.0 copy-start.3
  37.6 15.7 %all_to_all.21 = bf16[32,32,128]{2,1,0:T(8,128)(2,1)S(1)} all-to-all(bf16[32,32,128]{2,1,0:T(8,128)(2,1)S(1)} %totals.1), channel_id=1, replica_groups=mesh['x'=4,'z'=8,'y'=4,'core'=2] {'z','y'}, dimensions={0} | all-to-all | bytes 524288 | tf_op jit(solution)/shard_map/all_to_all | solution.py:430
  53.4 0.0 collective-permute-start.1
  53.4 0.0 copy-done.5
  53.4 1.5 %collective-permute-done.1.other_ref = bf16[1024,128]{1,0:T(8,128)(2,1)S(1)} collective-permute-done((bf16[1024,128]{1,0:T(8,128)(2,1)S(1)}, bf16[1024,128]{1,0:T(8,128)(2,1)S(1)}, u32[]{:S(2)}, u32[]{:S(2)}) %collective-permute-start.1) | collective-permute-done | bytes 262176 | tf_op jit(solution)/shard_map/ppermute | solution.py:432
  54.9 0.0 slice-done
  54.9 0.0 slice-done.1
  54.9 0.0 slice-done.2
  54.9 0.0 copy-done
  54.9 0.0 copy-done.1
  54.9 2.3 %tail_of.1 = (bf16[64,2240]{1,0:T(8,128)(2,1)S(1)}, bf16[64,2240]{1,0:T(8,128)(2,1)S(1)}) custom-call(s32[1]{0:T(128)S(6)} %copy.12.valid_ref, bf16[1024,128]{1,0:T(8,128)(2,1)S(1)} %bitcast.16, bf16[1024,128]{1,0:T(8,128)(2,1)S(1)} %collective-permute-done.1.other_ref, bf16[128,2240]{1,0:T(8,128)(2,1)S(1)} %bitcast.11, bf16[128,2240]{1,0:T(8,128)(2,1)S(1)} %bitcast.13, ...), custom_call_target="tpu_custom_call" | custom-call | flops 3000000000 | bytes 1048576 | tf_op jit(solution)/shard_map/tail_of/pallas_call | solution.py:321
  57.2 2.7 %collective-permute-start.2 = (bf16[64,2240]{1,0:T(8,128)(2,1)S(1)}, bf16[64,2240]{1,0:T(8,128)(2,1)S(1)}, u32[]{:S(2)}, u32[]{:S(2)}) collective-permute-start(bf16[64,2240]{1,0:T(8,128)(2,1)S(1)} %get-tuple-element.15.tail_normed), channel_id=1, source_target_pairs={{0,8},{8,16},{16,24},{24,32},{32,40},{40,48},{48,56},{56,64},{64,7... | collective-permute-start | bytes 860168 | tf_op jit(solution)/shard_map/ppermute | solution.py:436
  59.9 0.0 copy-done.3
  59.9 3.3 %head_of.1 = (bf16[128,2240]{1,0:T(8,128)(2,1)}, bf16[64,2240]{1,0:T(8,128)(2,1)S(1)}, f32[64,2240]{1,0:T(8,128)S(1)}) custom-call(s32[1]{0:T(128)S(6)} %copy.12.valid_ref, bf16[1024,128]{1,0:T(8,128)(2,1)S(1)} %bitcast.17, bf16[1024,128]{1,0:T(8,128)(2,1)S(1)} %collective-permute-done.1.other_ref, bf16[128,2240]{1,0:T(8,128)(2,1)S(1)} %bitcast.12, ...), custom_call_target="tpu_custom_call" | custom-call | flops 3000000000 | bytes 1048576 | tf_op jit(solution)/shard_map/head_of/pallas_call | solution.py:364
  63.2 7.1 %collective-permute-done.2.halo_ref = bf16[64,2240]{1,0:T(8,128)(2,1)S(1)} collective-permute-done((bf16[64,2240]{1,0:T(8,128)(2,1)S(1)}, bf16[64,2240]{1,0:T(8,128)(2,1)S(1)}, u32[]{:S(2)}, u32[]{:S(2)}) %collective-permute-start.2) | collective-permute-done | bytes 286752 | tf_op jit(solution)/shard_map/ppermute | solution.py:436
  70.3 0.9 %finish.1 = bf16[128,2240]{1,0:T(8,128)(2,1)} custom-call(bf16[128,2240]{1,0:T(8,128)(2,1)} %get-tuple-element.16.unused_ref, bf16[64,2240]{1,0:T(8,128)(2,1)S(1)} %get-tuple-element.17.residual_ref, f32[64,2240]{1,0:T(8,128)S(1)} %get-tuple-element.18.partial_ref, ...), custom_call_target="tpu_custom_call", output_to_operand_aliasing={{}: (0, {})} | custom-call | flops 1000000000 | bytes 1048576 | tf_op jit(solution)/shard_map/finish/pallas_call | solution.py:401
  (7 shorter events, 0.1 us)
Async XLA Ops:
  0.7 1.1 %copy-start.2 = (bf16[4,1,32,2240]{3,2,1,0:T(8,128)(2,1)S(1)}, bf16[4,1,32,2240]{3,2,1,0:T(8,128)(2,1)}, u32[]{:S(2)}) copy-start(bf16[4,1,32,2240]{3,2,1,0:T(8,128)(2,1)} %param.9) | copy-start | bytes 1720324
  0.7 1.3 %copy-start.4 = (bf16[4,1,32,2240]{3,2,1,0:T(8,128)(2,1)S(1)}, bf16[4,1,32,2240]{3,2,1,0:T(8,128)(2,1)}, u32[]{:S(2)}) copy-start(bf16[4,1,32,2240]{3,2,1,0:T(8,128)(2,1)} %param.10) | copy-start | bytes 1720324
  2.3 1.6 %collective-permute-start = (bf16[1024,128]{1,0:T(8,128)(2,1)S(1)}, bf16[1024,128]{1,0:T(8,128)(2,1)S(1)}, u32[]{:S(2)}, u32[]{:S(2)}) collective-permute-start(bf16[1024,128]{1,0:T(8,128)(2,1)S(1)} %sent_states.1), channel_id=1, source_target_pairs={{0,1},{1,0},{2,3},{3,2},{4,5},{5,4},{6,7},{7,6},{8,9},{9,8},{10,11... | collective-permute-start | bytes 786440 | tf_op jit(solution)/shard_map/ppermute | solution.py:423
  28.5 26.4 %slice-start = ((s8[10321920]{0:T(1024)(128)(4,1)}), s8[4194304]{0:T(1024)(128)(4,1)S(1)}, s32[]{:S(2)}) async-start(s8[10321920]{0:T(1024)(128)(4,1)} %bitcast.9), calls=%async_computation.3 | async-start | bytes 8388608
  28.5 26.4 %slice-start.1 = ((s8[10321920]{0:T(1024)(128)(4,1)}), s8[4194304]{0:T(1024)(128)(4,1)S(1)}, s32[]{:S(2)}) async-start(s8[10321920]{0:T(1024)(128)(4,1)} %bitcast.9), calls=%async_computation.4 | async-start | bytes 8388608
  37.6 15.8 %copy-start.5 = (f32[2240]{0:T(1024)S(1)}, f32[2240]{0:T(1024)}, u32[]{:S(2)}) copy-start(f32[2240]{0:T(1024)} %param.13) | copy-start | bytes 26884
  37.6 17.3 %slice-start.2 = ((s8[10321920]{0:T(1024)(128)(4,1)}), s8[1933312]{0:T(1024)(128)(4,1)S(1)}, s32[]{:S(2)}) async-start(s8[10321920]{0:T(1024)(128)(4,1)} %bitcast.9), calls=%async_computation.5 | async-start | bytes 3866624
  37.6 17.3 %copy-start = (bf16[4,1,32,2240]{3,2,1,0:T(8,128)(2,1)S(1)}, bf16[4,1,32,2240]{3,2,1,0:T(8,128)(2,1)}, u32[]{:S(2)}) copy-start(bf16[4,1,32,2240]{3,2,1,0:T(8,128)(2,1)} %param.8) | copy-start | bytes 1720324
  37.6 17.3 %copy-start.1 = (bf16[4,1,32,2240]{3,2,1,0:T(8,128)(2,1)S(1)}, bf16[4,1,32,2240]{3,2,1,0:T(8,128)(2,1)}, u32[]{:S(2)}) copy-start(bf16[4,1,32,2240]{3,2,1,0:T(8,128)(2,1)} %param.11) | copy-start | bytes 1720324
  37.6 22.3 %copy-start.3 = (f32[3,2240]{1,0:T(4,128)S(1)}, f32[3,2240]{1,0:T(4,128)}, u32[]{:S(2)}) copy-start(f32[3,2240]{1,0:T(4,128)} %taps_ref.3) | copy-start | bytes 80644
  53.4 1.5 %collective-permute-start.1 = (bf16[1024,128]{1,0:T(8,128)(2,1)S(1)}, bf16[1024,128]{1,0:T(8,128)(2,1)S(1)}, u32[]{:S(2)}, u32[]{:S(2)}) collective-permute-start(bf16[1024,128]{1,0:T(8,128)(2,1)S(1)} %bitcast.15), channel_id=1, source_target_pairs={{0,1},{1,0},{2,3},{3,2},{4,5},{5,4},{6,7},{7,6},{8,9},{9,8},{10,11... | collective-permute-start | bytes 786440 | tf_op jit(solution)/shard_map/ppermute | solution.py:432
  57.2 13.0 %collective-permute-start.2 = (bf16[64,2240]{1,0:T(8,128)(2,1)S(1)}, bf16[64,2240]{1,0:T(8,128)(2,1)S(1)}, u32[]{:S(2)}, u32[]{:S(2)}) collective-permute-start(bf16[64,2240]{1,0:T(8,128)(2,1)S(1)} %get-tuple-element.15.tail_normed), channel_id=1, source_target_pairs={{0,8},{8,16},{16,24},{24,32},{32,40},{40,48},{48,56},{56,64},{64,7... | collective-permute-start | bytes 860168 | tf_op jit(solution)/shard_map/ppermute | solution.py:436

commit v2 on v1

--- a/solution.py
+++ b/solution.py
@@ -18,6 +18,7 @@
 EPS_NORM = 1e-06
 X, Z, Y, C = 4, 8, 4, 2
 CHUNK = 512
+SPLIT = 1152
 
 
 def smem():
@@ -206,9 +207,7 @@
     )(prefix, whole)
 
 
-def project(
-    valid_ref, own_ref, other_ref, query_ref, hidden_ref, gain_ref, weight, first, attended, residual, normed_ref
-):
+def attend_rows(valid_ref, own_ref, other_ref, query_ref, first, attended):
     count, features = query_ref.shape
     step = count // 2
     own = lax.axis_index("core")
@@ -282,83 +281,126 @@
     if left:
         attended[:, features - left :] = carry[:, :left].astype(jnp.bfloat16)
 
+
+def project_columns(attended, hidden_ref, weight, residual, start, stop):
+    for s in range(start, stop, CHUNK):
+        at = slice(s, min(s + CHUNK, stop))
+        projected = jnp.dot(attended[...], weight[:, at], preferred_element_type=jnp.float32)
+        rounded = (hidden_ref[:, at].astype(jnp.float32) + projected).astype(jnp.bfloat16)
+        residual[:, at.start - start : at.stop - start] = rounded
+
+
+def inverse_of(parts):
+    count = parts[0].shape[0]
+    features = sum(part.shape[1] for part in parts)
     squares = jnp.zeros((count, LANES), jnp.float32)
-    for s in range(0, features, CHUNK):
-        w = min(CHUNK, features - s)
-        projected = jnp.dot(
-            attended[...], weight[:, s : s + w], preferred_element_type=jnp.float32
-        )
-        rounded = (hidden_ref[:, s : s + w].astype(jnp.float32) + projected).astype(jnp.bfloat16)
-        residual[:, s : s + w] = rounded
-        wide = rounded.astype(jnp.float32)
-        wide = wide * wide
-        for a in range(0, w, LANES):
-            b = min(LANES, w - a)
-            part = wide[:, a : a + b]
-            if b < LANES:
-                part = jnp.concatenate([part, jnp.zeros((count, LANES - b), jnp.float32)], axis=1)
-            squares = squares + part
+    for part in parts:
+        width = part.shape[1]
+        for s in range(0, width, LANES):
+            w = min(LANES, width - s)
+            wide = part[:, s : s + w].astype(jnp.float32)
+            wide = wide * wide
+            if w < LANES:
+                wide = jnp.concatenate([wide, jnp.zeros((count, LANES - w), jnp.float32)], axis=1)
+            squares = squares + wide
     mean = jnp.sum(squares, axis=1, keepdims=True) / features
-    inverse = jnp.broadcast_to(lax.rsqrt(mean + EPS_NORM), (count, LANES))
-    for s in range(0, features, LANES):
-        w = min(LANES, features - s)
-        here = residual[:, s : s + w].astype(jnp.float32)
-        normed = (here * inverse[:, :w] * gain_ref[:, s : s + w]).astype(jnp.bfloat16)
-        normed_ref[:, s : s + w] = normed
-
-
-def tail_kernel(valid_ref, own_ref, other_ref, query_ref, hidden_ref, gain_ref, weight, residual, normed_ref, attended):
+    return jnp.broadcast_to(lax.rsqrt(mean + EPS_NORM), (count, LANES))
+
+
+def normed_at(parts, inverse, gain_ref, s, w):
+    here = at_columns(parts, s, w)
+    normed = (here * inverse[:, :w] * gain_ref[:, s : s + w]).astype(jnp.bfloat16)
+    return normed.astype(jnp.float32)
+
+
+def at_columns(parts, s, w):
+    for part in parts:
+        if s < part.shape[1]:
+            return part[:, s : s + w].astype(jnp.float32)
+        s -= part.shape[1]
+
+
+def tail_a_kernel(
+    valid_ref, own_ref, other_ref, query_ref, hidden_ref, weight, attended, residual
+):
     half = query_ref.shape[0] // 2
-    project(
-        valid_ref, own_ref, other_ref, query_ref.at[half:, :], hidden_ref.at[half:, :],
-        gain_ref, weight, 2, attended, residual, normed_ref,
-    )
-
-
-def tail_of(valid, own, other, query, hidden, gain, weight):
+    attend_rows(valid_ref, own_ref, other_ref, query_ref.at[half:, :], 2, attended)
+    project_columns(attended, hidden_ref.at[half:, :], weight, residual, 0, SPLIT)
+
+
+def tail_a(valid, own, other, query, hidden, weight):
     tokens, features = query.shape
-    half = jax.ShapeDtypeStruct((tokens // 2, features), jnp.bfloat16)
-    return pl.pallas_call(
-        tail_kernel,
-        out_shape=(half, half),
-        in_specs=[smem()] + [vmem()] * 6,
+    return pl.pallas_call(
+        tail_a_kernel,
+        out_shape=(
+            jax.ShapeDtypeStruct((tokens // 2, features), jnp.bfloat16),
+            jax.ShapeDtypeStruct((tokens // 2, SPLIT), jnp.bfloat16),
+        ),
+        in_specs=[smem()] + [vmem()] * 5,
         out_specs=(vmem(), vmem()),
-        scratch_shapes=[pltpu.VMEM(half.shape, jnp.bfloat16)],
         compiler_params=limit(24),
         cost_estimate=cost(3),
-        name="tail_of",
-    )(valid, own, other, query, hidden, gain, weight)
+        name="tail_a",
+    )(valid, own, other, query, hidden, weight)
+
+
+def tail_b_kernel(attended, hidden_ref, weight, residual):
+    half, features = attended.shape
+    project_columns(attended, hidden_ref.at[half:, :], weight, residual, SPLIT, features)
+
+
+def tail_b(attended, hidden, weight):
+    half, features = attended.shape
+    return pl.pallas_call(
+        tail_b_kernel,
+        out_shape=jax.ShapeDtypeStruct((half, features - SPLIT), jnp.bfloat16),
+        in_specs=[vmem()] * 3,
+        out_specs=vmem(),
+        compiler_params=limit(24),
+        cost_estimate=cost(1),
+        name="tail_b",
+    )(attended, hidden, weight)
 
 
 def head_kernel(
-    valid_ref, own_ref, other_ref, query_ref, hidden_ref, gain_ref, weight,
-    tail_residual, tail_normed, taps_ref, out_ref, residual, partial_ref, attended, normed_ref
+    valid_ref,
+    own_ref,
+    other_ref,
+    query_ref,
+    hidden_ref,
+    weight,
+    gain_ref,
+    left_ref,
+    right_ref,
+    taps_ref,
+    out_ref,
+    residual,
+    partial_ref,
+    attended,
 ):
     count, features = residual.shape
     step = count // 2
-    project(
-        valid_ref, own_ref, other_ref, query_ref.at[:count, :], hidden_ref.at[:count, :],
-        gain_ref, weight, 0, attended, residual, normed_ref,
-    )
+    attend_rows(valid_ref, own_ref, other_ref, query_ref.at[:count, :], 0, attended)
+    project_columns(attended, hidden_ref.at[:count, :], weight, residual, 0, features)
+    head, tail = (residual,), (left_ref, right_ref)
+    head_inverse, tail_inverse = inverse_of(head), inverse_of(tail)
     for s in range(0, features, LANES):
         w = min(LANES, features - s)
         taps = [taps_ref[j : j + 1, s : s + w] for j in range(3)]
-        frames = [
-            ref[t * step : (t + 1) * step, s : s + w].astype(jnp.float32)
-            for ref in (normed_ref, tail_normed)
-            for t in range(2)
-        ]
+        early = normed_at(head, head_inverse, gain_ref, s, w)
+        late = normed_at(tail, tail_inverse, gain_ref, s, w)
+        frames = [early[:step], early[step:], late[:step], late[step:]]
         partial_ref[:step, s : s + w] = taps[0] * frames[0]
         partial_ref[step:, s : s + w] = taps[0] * frames[1] + taps[1] * frames[0]
+        here = at_columns(tail, s, w)
         for t in range(2):
             total = taps[0] * frames[t + 2] + taps[1] * frames[t + 1] + taps[2] * frames[t]
             temporal = total.astype(jnp.bfloat16).astype(jnp.float32)
             at = slice(t * step, (t + 1) * step)
-            here = tail_residual[at, s : s + w].astype(jnp.float32)
-            out_ref[at, s : s + w] = (here + temporal).astype(jnp.bfloat16)
-
-
-def head_of(valid, own, other, query, hidden, gain, weight, tail_residual, tail_normed, taps):
+            out_ref[at, s : s + w] = (here[at] + temporal).astype(jnp.bfloat16)
+
+
+def head_of(valid, own, other, query, hidden, weight, gain, left, right, taps):
     tokens, features = query.shape
     half = (tokens // 2, features)
     return pl.pallas_call(
@@ -371,21 +413,25 @@
         ),
         in_specs=[smem()] + [vmem()] * 9,
         out_specs=(pl.BlockSpec(half, lambda i: (1, 0)), vmem(), vmem()),
-        scratch_shapes=[pltpu.VMEM(half, jnp.bfloat16), pltpu.VMEM(half, jnp.bfloat16)],
+        scratch_shapes=[pltpu.VMEM(half, jnp.bfloat16)],
         compiler_params=limit(24),
         cost_estimate=cost(3),
         name="head_of",
-    )(valid, own, other, query, hidden, gain, weight, tail_residual, tail_normed, taps)
-
-
-def finish_kernel(unused_ref, residual_ref, partial_ref, halo_ref, taps_ref, out_ref):
+    )(valid, own, other, query, hidden, weight, gain, left, right, taps)
+
+
+def finish_kernel(
+    unused_ref, residual_ref, partial_ref, left_ref, right_ref, gain_ref, taps_ref, out_ref
+):
     count, features = residual_ref.shape
     step = count // 2
+    halo = (left_ref, right_ref)
+    inverse = inverse_of(halo)
     for s in range(0, features, LANES):
         w = min(LANES, features - s)
         taps = [taps_ref[j : j + 1, s : s + w] for j in range(3)]
-        oldest = halo_ref[:step, s : s + w].astype(jnp.float32)
-        older = halo_ref[step:, s : s + w].astype(jnp.float32)
+        before = normed_at(halo, inverse, gain_ref, s, w)
+        oldest, older = before[:step], before[step:]
         totals = [
             partial_ref[:step, s : s + w] + taps[1] * older + taps[2] * oldest,
             partial_ref[step:, s : s + w] + taps[2] * older,
@@ -397,18 +443,18 @@
             out_ref[at, s : s + w] = (here + temporal).astype(jnp.bfloat16)
 
 
-def finish(out, residual, partial, halo, taps):
+def finish(out, residual, partial, left, right, gain, taps):
     return pl.pallas_call(
         finish_kernel,
         grid=(1,),
         out_shape=jax.ShapeDtypeStruct(out.shape, out.dtype),
-        in_specs=[pl.BlockSpec(memory_space=pl.ANY)] + [vmem()] * 4,
+        in_specs=[pl.BlockSpec(memory_space=pl.ANY)] + [vmem()] * 6,
         out_specs=pl.BlockSpec(residual.shape, lambda i: (0, 0)),
         input_output_aliases={0: 0},
         compiler_params=limit(8),
         cost_estimate=cost(1),
         name="finish",
-    )(out, residual, partial, halo, taps)
+    )(out, residual, partial, left, right, gain, taps)
 
 
 def body(query_in, key_in, value_in, hidden_in, out_weight, norm_gain, temporal_taps, block_valid):
@@ -431,11 +477,14 @@
     own = own.reshape(ROWS, LANES)
     other = lax.ppermute(own, "core", swap)
     gain = norm_gain.reshape(1, features)
-    shared = (block_valid, own, other, query, hidden, gain, out_weight)
-    tail_residual, tail_normed = tail_of(*shared)
-    halo = lax.ppermute(tail_normed, ("x", "z"), [(i, i + 1) for i in range(X * Z - 1)])
-    out, residual, partial = head_of(*shared, tail_residual, tail_normed, temporal_taps)
-    mixed = finish(out, residual, partial, halo, temporal_taps)
+    shared = (block_valid, own, other, query, hidden, out_weight)
+    chain = [(i, i + 1) for i in range(X * Z - 1)]
+    attended, left = tail_a(*shared)
+    halo_left = lax.ppermute(left, ("x", "z"), chain)
+    right = tail_b(attended, hidden, out_weight)
+    halo_right = lax.ppermute(right, ("x", "z"), chain)
+    out, residual, partial = head_of(*shared, gain, left, right, temporal_taps)
+    mixed = finish(out, residual, partial, halo_left, halo_right, gain, temporal_taps)
     return mixed.reshape(query_in.shape)
 
 

time: 71.4 us -> 71.7 us (level)
  starting transfers between devices: 2.77 us -> 5.25 us
  waiting for transfers between devices: 9.74 us -> 7.27 us
    ppermute x1 -> x2, starting transfers between devices: 2.67 us -> 5.15 us  [the longest x1 2.68 us: body(): halo_right = lax.ppermute(right, ('x', 'z'), chain)]
    ppermute x1 -> x2, waiting for transfers between devices: 7.08 us -> 4.61 us  [the longest x1 2.41 us: body(): halo_left = lax.ppermute(left, ('x', 'z'), chain)]
    pallas_call x1 -> x2, Pallas kernels: 2.27 us -> 2.35 us  [the longest x1 1.32 us: tail_a(): pl.pallas_call(tail_a_kernel, out_shape=(jax.ShapeDtypeStruct((tokens //...]
  transfers between devices with their start and end apart: 3 -> 4, of which waited for: 3 -> 4; matrix products, arithmetic and copies ran while one was open for 0% -> 0% of each run, Pallas kernels for 5% -> 5%
where the time goes in v2:
time: 71.7 us; the launch traced here: 71.4 us
  blocking collectives  49.3 us (69%)
  Pallas kernels  7.66 us (11%)
  waiting for transfers between devices  7.27 us (10%)
  starting transfers between devices  5.25 us (7%)
  local copies, waits for them, and re-layouts  1.06 us (1%)
  between operations  0.8 us (1%)
    all_to_all x1, blocking collectives, body(): lax.all_to_all(mine, ('z', 'y'), 0, 0, tiled=True)  24.5 us
    all_to_all x1, blocking collectives, body(): own = lax.all_to_all(totals(prefix, wholes), ('z', 'y'), 0, 0, tiled=True)  15.7 us
    all_to_all x1, blocking collectives, body(): wholes = lax.all_to_all(whole, 'x', 0, 0, tiled=True)  9.06 us
    pallas_call x1, Pallas kernels, head_of(): pl.pallas_call(head_kernel, grid=(1,), out_shape=(jax.ShapeDtypeStruct(qu...  3.26 us
    ppermute x1, starting transfers between devices, body(): halo_right = lax.ppermute(right, ('x', 'z'), chain)  2.68 us
    ppermute x1, starting transfers between devices, body(): halo_left = lax.ppermute(left, ('x', 'z'), chain)  2.47 us
    ppermute x1, waiting for transfers between devices, body(): halo_left = lax.ppermute(left, ('x', 'z'), chain)  2.41 us
    ppermute x1, waiting for transfers between devices, body(): halo_right = lax.ppermute(right, ('x', 'z'), chain)  2.2 us
  transfers between devices with their start and end apart: 4, of which 4 were waited for; matrix products, arithmetic and copies ran while one was open for 0% of the time, Pallas kernels for 5%

profile of v2, /device:TPU:2, one launch (start us, length us, event | category | flops | bytes accessed | tf_op | source)
XLA Modules:
  0.0 71.4 jit_solution(17226005463819058189)
XLA Ops:
  0.7 0.0 copy-start.2
  0.7 0.0 copy-start.4
  0.7 1.0 %copy-done.2 = bf16[4,1,32,2240]{3,2,1,0:T(8,128)(2,1)S(1)} copy-done((bf16[4,1,32,2240]{3,2,1,0:T(8,128)(2,1)S(1)}, bf16[4,1,32,2240]{3,2,1,0:T(8,128)(2,1)}, u32[]{:S(2)}) %copy-start.2) | copy-done | bytes 573464
  1.7 0.2 turn.1.turned
  1.9 0.0 copy-done.4
  1.9 0.3 sent_states.1
  2.3 0.1 collective-permute-start
  2.4 0.4 kept_states.1
  2.7 1.1 %collective-permute-done = bf16[1024,128]{1,0:T(8,128)(2,1)S(1)} collective-permute-done((bf16[1024,128]{1,0:T(8,128)(2,1)S(1)}, bf16[1024,128]{1,0:T(8,128)(2,1)S(1)}, u32[]{:S(2)}, u32[]{:S(2)}) %collective-permute-start) | collective-permute-done | bytes 262176 | tf_op jit(solution)/shard_map/ppermute | solution.py:469
  3.9 0.1 add_convert_fusion
  3.9 24.5 %all_to_all.19.got_ref = bf16[32,32,128]{2,1,0:T(8,128)(2,1)S(1)} all-to-all(bf16[32,32,128]{2,1,0:T(8,128)(2,1)S(1)} %bitcast.22), channel_id=1, replica_groups=mesh['x'=4,'z'=8,'y'=4,'core'=2] {'z','y'}, dimensions={0} | all-to-all | bytes 524288 | tf_op jit(solution)/shard_map/all_to_all | solution.py:473
  28.5 0.0 slice-start
  28.5 9.1 %all_to_all.20.whole_ref = f32[4,32,128]{2,1,0:T(8,128)S(1)} all-to-all(f32[4,32,128]{2,1,0:T(8,128)S(1)} %get-tuple-element.13), channel_id=1, replica_groups=mesh['x'=4,'z'=8,'y'=4,'core'=2] {'x'}, dimensions={0} | all-to-all | bytes 131072 | tf_op jit(solution)/shard_map/all_to_all | solution.py:475
  37.6 15.7 %all_to_all.21 = bf16[32,32,128]{2,1,0:T(8,128)(2,1)S(1)} all-to-all(bf16[32,32,128]{2,1,0:T(8,128)(2,1)S(1)} %totals.1), channel_id=1, replica_groups=mesh['x'=4,'z'=8,'y'=4,'core'=2] {'z','y'}, dimensions={0} | all-to-all | bytes 524288 | tf_op jit(solution)/shard_map/all_to_all | solution.py:476
  53.4 0.0 collective-permute-start.1
  53.4 0.0 copy-done.5
  53.4 1.5 %collective-permute-done.1.other_ref = bf16[1024,128]{1,0:T(8,128)(2,1)S(1)} collective-permute-done((bf16[1024,128]{1,0:T(8,128)(2,1)S(1)}, bf16[1024,128]{1,0:T(8,128)(2,1)S(1)}, u32[]{:S(2)}, u32[]{:S(2)}) %collective-permute-start.1) | collective-permute-done | bytes 262176 | tf_op jit(solution)/shard_map/ppermute | solution.py:478
  54.9 0.0 slice-done
  54.9 0.0 slice-done.1
  54.9 0.0 slice-done.2
  54.9 0.0 copy-done
  54.9 0.0 copy-done.1
  54.9 0.0 copy-start.3
  54.9 1.3 %tail_a.1 = (bf16[64,2240]{1,0:T(8,128)(2,1)S(1)}, bf16[64,1152]{1,0:T(8,128)(2,1)S(1)}) custom-call(s32[1]{0:T(128)S(6)} %copy.12.valid_ref, bf16[1024,128]{1,0:T(8,128)(2,1)S(1)} %bitcast.15, bf16[1024,128]{1,0:T(8,128)(2,1)S(1)} %collective-permute-done.1.other_ref, bf16[128,2240]{1,0:T(8,128)(2,1)S(1)} %bitcast.17, bf16[128,2240]{1,0:T(8,128)(2,1)S(1)} %bitcast.11, ...), custom_call_target="tpu_custom_call" | custom-call | flops 3000000000 | bytes 1048576 | tf_op jit(solution)/shard_map/tail_a/pallas_call | solution.py:333
  56.3 1.0 %tail_b.1.right_ref = bf16[64,1088]{1,0:T(8,128)(2,1)S(1)} custom-call(bf16[64,2240]{1,0:T(8,128)(2,1)S(1)} %get-tuple-element.15.attended, bf16[128,2240]{1,0:T(8,128)(2,1)S(1)} %bitcast.12, bf16[2240,2240]{1,0:T(8,128)(2,1)S(1)} %bitcast.10), custom_call_target="tpu_custom_call" | custom-call | flops 1000000000 | bytes 1048576 | tf_op jit(solution)/shard_map/tail_b/pallas_call | solution.py:354
  57.3 2.7 %collective-permute-start.3 = (bf16[64,1088]{1,0:T(8,128)(2,1)S(1)}, bf16[64,1088]{1,0:T(8,128)(2,1)S(1)}, u32[]{:S(2)}, u32[]{:S(2)}) collective-permute-start(bf16[64,1088]{1,0:T(8,128)(2,1)S(1)} %tail_b.1.right_ref), channel_id=1, source_target_pairs={{0,8},{8,16},{16,24},{24,32},{32,40},{40,48},{48,56},{56,64},{64,7... | collective-permute-start | bytes 417800 | tf_op jit(solution)/shard_map/ppermute | solution.py:485
  60.0 2.5 %collective-permute-start.2 = (bf16[64,1152]{1,0:T(8,128)(2,1)S(1)}, bf16[64,1152]{1,0:T(8,128)(2,1)S(1)}, u32[]{:S(2)}, u32[]{:S(2)}) collective-permute-start(bf16[64,1152]{1,0:T(8,128)(2,1)S(1)} %get-tuple-element.14.left_ref), channel_id=1, source_target_pairs={{0,8},{8,16},{16,24},{24,32},{32,40},{40,48},{48,56},{56,64},{64,7... | collective-permute-start | bytes 442376 | tf_op jit(solution)/shard_map/ppermute | solution.py:483
  62.5 0.0 copy-done.3
  62.5 3.3 %head_of.1 = (bf16[128,2240]{1,0:T(8,128)(2,1)}, bf16[64,2240]{1,0:T(8,128)(2,1)S(1)}, f32[64,2240]{1,0:T(8,128)S(1)}) custom-call(s32[1]{0:T(128)S(6)} %copy.12.valid_ref, bf16[1024,128]{1,0:T(8,128)(2,1)S(1)} %bitcast.16, bf16[1024,128]{1,0:T(8,128)(2,1)S(1)} %collective-permute-done.1.other_ref, bf16[128,2240]{1,0:T(8,128)(2,1)S(1)} %bitcast.18, ...), custom_call_target="tpu_custom_call" | custom-call | flops 3000000000 | bytes 1048576 | tf_op jit(solution)/shard_map/head_of/pallas_call | solution.py:406
  65.7 2.2 %collective-permute-done.3.right_ref = bf16[64,1088]{1,0:T(8,128)(2,1)S(1)} collective-permute-done((bf16[64,1088]{1,0:T(8,128)(2,1)S(1)}, bf16[64,1088]{1,0:T(8,128)(2,1)S(1)}, u32[]{:S(2)}, u32[]{:S(2)}) %collective-permute-start.3) | collective-permute-done | bytes 139296 | tf_op jit(solution)/shard_map/ppermute | solution.py:485
  67.9 2.4 %collective-permute-done.2.left_ref = bf16[64,1152]{1,0:T(8,128)(2,1)S(1)} collective-permute-done((bf16[64,1152]{1,0:T(8,128)(2,1)S(1)}, bf16[64,1152]{1,0:T(8,128)(2,1)S(1)}, u32[]{:S(2)}, u32[]{:S(2)}) %collective-permute-start.2) | collective-permute-done | bytes 147488 | tf_op jit(solution)/shard_map/ppermute | solution.py:483
  70.4 1.1 %finish.1 = bf16[128,2240]{1,0:T(8,128)(2,1)} custom-call(bf16[128,2240]{1,0:T(8,128)(2,1)} %get-tuple-element.16.unused_ref, bf16[64,2240]{1,0:T(8,128)(2,1)S(1)} %get-tuple-element.17.residual_ref, f32[64,2240]{1,0:T(8,128)S(1)} %get-tuple-element.18.partial_ref, ...), custom_call_target="tpu_custom_call", output_to_operand_aliasing={{}: (0, {})} | custom-call | flops 1000000000 | bytes 1048576 | tf_op jit(solution)/shard_map/finish/pallas_call | solution.py:447
  (10 shorter events, 0.1 us)
Async XLA Ops:
  0.7 1.1 %copy-start.2 = (bf16[4,1,32,2240]{3,2,1,0:T(8,128)(2,1)S(1)}, bf16[4,1,32,2240]{3,2,1,0:T(8,128)(2,1)}, u32[]{:S(2)}) copy-start(bf16[4,1,32,2240]{3,2,1,0:T(8,128)(2,1)} %param.9) | copy-start | bytes 1720324
  0.7 1.3 %copy-start.4 = (bf16[4,1,32,2240]{3,2,1,0:T(8,128)(2,1)S(1)}, bf16[4,1,32,2240]{3,2,1,0:T(8,128)(2,1)}, u32[]{:S(2)}) copy-start(bf16[4,1,32,2240]{3,2,1,0:T(8,128)(2,1)} %param.10) | copy-start | bytes 1720324
  2.3 1.6 %collective-permute-start = (bf16[1024,128]{1,0:T(8,128)(2,1)S(1)}, bf16[1024,128]{1,0:T(8,128)(2,1)S(1)}, u32[]{:S(2)}, u32[]{:S(2)}) collective-permute-start(bf16[1024,128]{1,0:T(8,128)(2,1)S(1)} %sent_states.1), channel_id=1, source_target_pairs={{0,1},{1,0},{2,3},{3,2},{4,5},{5,4},{6,7},{7,6},{8,9},{9,8},{10,11... | collective-permute-start | bytes 786440 | tf_op jit(solution)/shard_map/ppermute | solution.py:469
  28.5 26.4 %slice-start = ((s8[10321920]{0:T(1024)(128)(4,1)}), s8[4194304]{0:T(1024)(128)(4,1)S(1)}, s32[]{:S(2)}) async-start(s8[10321920]{0:T(1024)(128)(4,1)} %bitcast.9), calls=%async_computation.3 | async-start | bytes 8388608
  28.5 26.4 %slice-start.1 = ((s8[10321920]{0:T(1024)(128)(4,1)}), s8[4194304]{0:T(1024)(128)(4,1)S(1)}, s32[]{:S(2)}) async-start(s8[10321920]{0:T(1024)(128)(4,1)} %bitcast.9), calls=%async_computation.4 | async-start | bytes 8388608
  37.6 15.8 %copy-start.5 = (f32[2240]{0:T(1024)S(1)}, f32[2240]{0:T(1024)}, u32[]{:S(2)}) copy-start(f32[2240]{0:T(1024)} %param.13) | copy-start | bytes 26884
  37.6 17.3 %slice-start.2 = ((s8[10321920]{0:T(1024)(128)(4,1)}), s8[1933312]{0:T(1024)(128)(4,1)S(1)}, s32[]{:S(2)}) async-start(s8[10321920]{0:T(1024)(128)(4,1)} %bitcast.9), calls=%async_computation.5 | async-start | bytes 3866624
  37.6 17.3 %copy-start = (bf16[4,1,32,2240]{3,2,1,0:T(8,128)(2,1)S(1)}, bf16[4,1,32,2240]{3,2,1,0:T(8,128)(2,1)}, u32[]{:S(2)}) copy-start(bf16[4,1,32,2240]{3,2,1,0:T(8,128)(2,1)} %param.11) | copy-start | bytes 1720324
  37.6 17.3 %copy-start.1 = (bf16[4,1,32,2240]{3,2,1,0:T(8,128)(2,1)S(1)}, bf16[4,1,32,2240]{3,2,1,0:T(8,128)(2,1)}, u32[]{:S(2)}) copy-start(bf16[4,1,32,2240]{3,2,1,0:T(8,128)(2,1)} %param.8) | copy-start | bytes 1720324
  53.4 1.5 %collective-permute-start.1 = (bf16[1024,128]{1,0:T(8,128)(2,1)S(1)}, bf16[1024,128]{1,0:T(8,128)(2,1)S(1)}, u32[]{:S(2)}, u32[]{:S(2)}) collective-permute-start(bf16[1024,128]{1,0:T(8,128)(2,1)S(1)} %bitcast.14), channel_id=1, source_target_pairs={{0,1},{1,0},{2,3},{3,2},{4,5},{5,4},{6,7},{7,6},{8,9},{9,8},{10,11... | collective-permute-start | bytes 786440 | tf_op jit(solution)/shard_map/ppermute | solution.py:478
  54.9 7.5 %copy-start.3 = (f32[3,2240]{1,0:T(4,128)S(1)}, f32[3,2240]{1,0:T(4,128)}, u32[]{:S(2)}) copy-start(f32[3,2240]{1,0:T(4,128)} %taps_ref.3) | copy-start | bytes 80644
  57.3 10.6 %collective-permute-start.3 = (bf16[64,1088]{1,0:T(8,128)(2,1)S(1)}, bf16[64,1088]{1,0:T(8,128)(2,1)S(1)}, u32[]{:S(2)}, u32[]{:S(2)}) collective-permute-start(bf16[64,1088]{1,0:T(8,128)(2,1)S(1)} %tail_b.1.right_ref), channel_id=1, source_target_pairs={{0,8},{8,16},{16,24},{24,32},{32,40},{40,48},{48,56},{56,64},{64,7... | collective-permute-start | bytes 417800 | tf_op jit(solution)/shard_map/ppermute | solution.py:485
  60.0 10.4 %collective-permute-start.2 = (bf16[64,1152]{1,0:T(8,128)(2,1)S(1)}, bf16[64,1152]{1,0:T(8,128)(2,1)S(1)}, u32[]{:S(2)}, u32[]{:S(2)}) collective-permute-start(bf16[64,1152]{1,0:T(8,128)(2,1)S(1)} %get-tuple-element.14.left_ref), channel_id=1, source_target_pairs={{0,8},{8,16},{16,24},{24,32},{32,40},{40,48},{48,56},{56,64},{64,7... | collective-permute-start | bytes 442376 | tf_op jit(solution)/shard_map/ppermute | solution.py:483

commit v3 on v2

--- a/solution.py
+++ b/solution.py
@@ -18,7 +18,7 @@
 EPS_NORM = 1e-06
 X, Z, Y, C = 4, 8, 4, 2
 CHUNK = 512
-SPLIT = 1152
+SPLIT = 1408
 
 
 def smem():
@@ -207,79 +207,134 @@
     )(prefix, whole)
 
 
-def attend_rows(valid_ref, own_ref, other_ref, query_ref, first, attended):
-    count, features = query_ref.shape
-    step = count // 2
-    own = lax.axis_index("core")
+def unpack(group, stored):
+    lanes = lane_of((DH, LANES))
+    packed = [stored(group, p) for p in range(GROUP - 1)]
+    end = group * GROUP + GROUP - 1
+    off = place_of(end)[1]
+    last = jnp.zeros((DH, LANES), jnp.float32)
+    for p in range(GROUP - 1):
+        free = free_of(group * GROUP + p)
+        if p < 8:
+            shift = (off + PIECE * p - free - 2) % LANES
+            start = (off + PIECE * p) % LANES
+            mask = (lanes >= start) & (lanes < start + PIECE)
+            if start + PIECE > LANES:
+                mask = mask | (lanes < start + PIECE - LANES)
+        else:
+            shift = (free_of(end) - free - 1) % LANES
+            mask = lanes == free_of(end)
+        wide = packed[p].astype(jnp.float32)
+        moved = pltpu.roll(wide, shift, axis=1) if shift else wide
+        last = jnp.where(mask, moved, last)
+    return packed + [last.astype(jnp.bfloat16)]
+
+
+def window(h, packed):
     lanes = lane_of((DH, LANES))
     zero = jnp.zeros((DH, LANES), jnp.bfloat16)
+    off = place_of(h)[1]
+    if off == 0:
+        return jnp.where(lanes <= DH, packed, zero)
+    low = jnp.where(lanes >= off, packed, zero)
+    high = jnp.where(lanes <= off - 16, packed, zero)
+    return jnp.concatenate([low, high], axis=1)
+
+
+def attend_group(group, stored, query_ref, live, attended, carry):
+    count, features = query_ref.shape
+    lane = lane_of((count, LANES))
+    unpacked = unpack(group, stored)
+    for p in range(GROUP):
+        h = group * GROUP + p
+        tile, off = place_of(h)
+        start = tile * LANES
+        stop = min(start + (LANES if off == 0 else 2 * LANES), features)
+        wide = window(h, unpacked[p])
+        parts = [wide]
+        if off:
+            parts.insert(0, jnp.zeros((off, wide.shape[1]), jnp.bfloat16))
+        rest = stop - start - off - DH
+        if rest:
+            parts.append(jnp.zeros((rest, wide.shape[1]), jnp.bfloat16))
+        matrix = jnp.concatenate(parts, axis=0) if len(parts) > 1 else wide
+        query = jnp.maximum(query_ref[:, start:stop], 0)
+        got = jnp.dot(query, matrix, preferred_element_type=jnp.float32)
+        below = got[:, off + DH : off + DH + 1] + EPS_DEN
+        scale = jnp.broadcast_to(live / below, (count, LANES))
+        low = got[:, :LANES] * scale
+        if off == 0:
+            carry = low
+            continue
+        full = jnp.where(lane >= off, low, carry)
+        attended[:, start : start + LANES] = full.astype(jnp.bfloat16)
+        carry = got[:, LANES:] * scale
+    return carry
+
+
+def live_rows(valid_ref, count, first):
+    step = count // 2
+    row = lax.broadcasted_iota(jnp.int32, (count, 1), 0)
+    return (row + first * step < valid_ref[0] * step).astype(jnp.float32)
+
+
+def store_end(attended, carry):
+    left = attended.shape[1] % LANES
+    if left:
+        attended[:, attended.shape[1] - left :] = carry[:, :left].astype(jnp.bfloat16)
+
+
+def attend_rows(valid_ref, own_ref, other_ref, query_ref, first, attended):
+    own = lax.axis_index("core")
 
     def stored(group, p):
         at = slice(p * DH, (p + 1) * DH)
         return jnp.where(own == group, own_ref[at, :], other_ref[at, :])
 
-    def unpack(group):
-        packed = [stored(group, p) for p in range(GROUP - 1)]
-        end = group * GROUP + GROUP - 1
-        off = place_of(end)[1]
-        last = jnp.zeros((DH, LANES), jnp.float32)
-        for p in range(GROUP - 1):
-            free = free_of(group * GROUP + p)
-            if p < 8:
-                shift = (off + PIECE * p - free - 2) % LANES
-                start = (off + PIECE * p) % LANES
-                mask = (lanes >= start) & (lanes < start + PIECE)
-                if start + PIECE > LANES:
-                    mask = mask | (lanes < start + PIECE - LANES)
-            else:
-                shift = (free_of(end) - free - 1) % LANES
-                mask = lanes == free_of(end)
-            wide = packed[p].astype(jnp.float32)
-            moved = pltpu.roll(wide, shift, axis=1) if shift else wide
-            last = jnp.where(mask, moved, last)
-        return packed + [last.astype(jnp.bfloat16)]
-
-    def window(h, packed):
-        off = place_of(h)[1]
-        if off == 0:
-            return jnp.where(lanes <= DH, packed, zero)
-        low = jnp.where(lanes >= off, packed, zero)
-        high = jnp.where(lanes <= off - 16, packed, zero)
-        return jnp.concatenate([low, high], axis=1)
-
-    row = lax.broadcasted_iota(jnp.int32, (count, 1), 0)
-    live = (row + first * step < valid_ref[0] * step).astype(jnp.float32)
-    lane = lane_of((count, LANES))
+    live = live_rows(valid_ref, query_ref.shape[0], first)
     carry = None
     for group in range(2):
-        unpacked = unpack(group)
-        for p in range(GROUP):
-            h = group * GROUP + p
-            tile, off = place_of(h)
-            start = tile * LANES
-            stop = min(start + (LANES if off == 0 else 2 * LANES), features)
-            wide = window(h, unpacked[p])
-            parts = [wide]
-            if off:
-                parts.insert(0, jnp.zeros((off, wide.shape[1]), jnp.bfloat16))
-            rest = stop - start - off - DH
-            if rest:
-                parts.append(jnp.zeros((rest, wide.shape[1]), jnp.bfloat16))
-            matrix = jnp.concatenate(parts, axis=0) if len(parts) > 1 else wide
-            query = jnp.maximum(query_ref[:, start:stop], 0)
-            got = jnp.dot(query, matrix, preferred_element_type=jnp.float32)
-            below = got[:, off + DH : off + DH + 1] + EPS_DEN
-            scale = jnp.broadcast_to(live / below, (count, LANES))
-            low = got[:, :LANES] * scale
-            if off == 0:
-                carry = low
-                continue
-            full = jnp.where(lane >= off, low, carry)
-            attended[:, start : start + LANES] = full.astype(jnp.bfloat16)
-            carry = got[:, LANES:] * scale
-    left = features % LANES
-    if left:
-        attended[:, features - left :] = carry[:, :left].astype(jnp.bfloat16)
+        carry = attend_group(group, stored, query_ref, live, attended, carry)
+    store_end(attended, carry)
+
+
+def attend_half(group, valid_ref, state_ref, query_ref, attended):
+    count = query_ref.shape[0]
+
+    def stored(group, p):
+        return state_ref[p * DH : (p + 1) * DH, :]
+
+    live = live_rows(valid_ref, count, 2)
+    carry = jnp.zeros((count, LANES), jnp.float32)
+    carry = attend_group(group, stored, query_ref, live, attended, carry)
+    if group:
+        store_end(attended, carry)
+    else:
+        tile = place_of(GROUP)[0] * LANES
+        attended[:, tile : tile + LANES] = carry.astype(jnp.bfloat16)
+
+
+def tail_own_kernel(valid_ref, own_ref, query_ref, attended):
+    half = query_ref.shape[0] // 2
+    core = lax.axis_index("core")
+    for group in range(2):
+
+        @pl.when(core == group)
+        def _():
+            attend_half(group, valid_ref, own_ref, query_ref.at[half:, :], attended)
+
+
+def tail_own(valid, own, query):
+    tokens, features = query.shape
+    return pl.pallas_call(
+        tail_own_kernel,
+        out_shape=jax.ShapeDtypeStruct((tokens // 2, features), jnp.bfloat16),
+        in_specs=[smem(), vmem(), vmem()],
+        out_specs=vmem(),
+        compiler_params=limit(8),
+        cost_estimate=cost(1),
+        name="tail_own",
+    )(valid, own, query)
 
 
 def project_columns(attended, hidden_ref, weight, residual, start, stop):
@@ -321,14 +376,28 @@
 
 
 def tail_a_kernel(
-    valid_ref, own_ref, other_ref, query_ref, hidden_ref, weight, attended, residual
+    valid_ref, other_ref, query_ref, hidden_ref, weight, own_attended, attended, residual
 ):
-    half = query_ref.shape[0] // 2
-    attend_rows(valid_ref, own_ref, other_ref, query_ref.at[half:, :], 2, attended)
-    project_columns(attended, hidden_ref.at[half:, :], weight, residual, 0, SPLIT)
-
-
-def tail_a(valid, own, other, query, hidden, weight):
+    count, features = attended.shape
+    core = lax.axis_index("core")
+    tile, off = place_of(GROUP)
+    shared = slice(tile * LANES, (tile + 1) * LANES)
+    lane = lane_of((count, LANES))
+    for group in range(2):
+
+        @pl.when(core == 1 - group)
+        def _():
+            attend_half(group, valid_ref, other_ref, query_ref.at[count:, :], attended)
+            done = slice(shared.stop, features) if group == 0 else slice(0, shared.start)
+            attended[:, done] = own_attended[:, done]
+            first = (attended if group == 0 else own_attended)[:, shared]
+            second = (own_attended if group == 0 else attended)[:, shared]
+            attended[:, shared] = jnp.where(lane < off, first, second)
+
+    project_columns(attended, hidden_ref.at[count:, :], weight, residual, 0, SPLIT)
+
+
+def tail_a(valid, other, query, hidden, weight, own_attended):
     tokens, features = query.shape
     return pl.pallas_call(
         tail_a_kernel,
@@ -341,7 +410,7 @@
         compiler_params=limit(24),
         cost_estimate=cost(3),
         name="tail_a",
-    )(valid, own, other, query, hidden, weight)
+    )(valid, other, query, hidden, weight, own_attended)
 
 
 def tail_b_kernel(attended, hidden_ref, weight, residual):
@@ -476,10 +545,11 @@
     own = lax.all_to_all(totals(prefix, wholes), ("z", "y"), 0, 0, tiled=True)
     own = own.reshape(ROWS, LANES)
     other = lax.ppermute(own, "core", swap)
+    own_attended = tail_own(block_valid, own, query)
     gain = norm_gain.reshape(1, features)
     shared = (block_valid, own, other, query, hidden, out_weight)
     chain = [(i, i + 1) for i in range(X * Z - 1)]
-    attended, left = tail_a(*shared)
+    attended, left = tail_a(block_valid, other, query, hidden, out_weight, own_attended)
     halo_left = lax.ppermute(left, ("x", "z"), chain)
     right = tail_b(attended, hidden, out_weight)
     halo_right = lax.ppermute(right, ("x", "z"), chain)

time: 71.7 us -> 71.6 us (level)
    ppermute x1, waiting for transfers between devices: 2.2 us -> 0.79 us  [body(): halo_right = lax.ppermute(right, ('x', 'z'), chain)]
    ppermute x1, waiting for transfers between devices: 2.41 us -> 3.81 us  [body(): halo_left = lax.ppermute(left, ('x', 'z'), chain)]
  transfers between devices with their start and end apart: 4 -> 4, of which waited for: 4 -> 4; matrix products, arithmetic and copies ran while one was open for 0% -> 0% of each run, Pallas kernels for 5% -> 6%
where the time goes in v3:
time: 71.6 us; the launch traced here: 71.4 us
  blocking collectives  49.3 us (69%)
  Pallas kernels  8.04 us (11%)
  waiting for transfers between devices  6.87 us (10%)
  starting transfers between devices  5.25 us (7%)
  local copies, waits for them, and re-layouts  1.06 us (1%)
  between operations  0.82 us (1%)
    all_to_all x1, blocking collectives, body(): lax.all_to_all(mine, ('z', 'y'), 0, 0, tiled=True)  24.5 us
    all_to_all x1, blocking collectives, body(): own = lax.all_to_all(totals(prefix, wholes), ('z', 'y'), 0, 0, tiled=True)  15.7 us
    all_to_all x1, blocking collectives, body(): wholes = lax.all_to_all(whole, 'x', 0, 0, tiled=True)  9.06 us
    ppermute x1, waiting for transfers between devices, body(): halo_left = lax.ppermute(left, ('x', 'z'), chain)  3.81 us
    pallas_call x1, Pallas kernels, head_of(): pl.pallas_call(head_kernel, grid=(1,), out_shape=(jax.ShapeDtypeStruct(qu...  3.25 us
    ppermute x1, starting transfers between devices, body(): halo_right = lax.ppermute(right, ('x', 'z'), chain)  2.67 us
    ppermute x1, starting transfers between devices, body(): halo_left = lax.ppermute(left, ('x', 'z'), chain)  2.48 us
    pallas_call x1, Pallas kernels, tail_a(): pl.pallas_call(tail_a_kernel, out_shape=(jax.ShapeDtypeStruct((tokens //...  1.57 us
  transfers between devices with their start and end apart: 4, of which 4 were waited for; matrix products, arithmetic and copies ran while one was open for 0% of the time, Pallas kernels for 6%

profile of v3, /device:TPU:2, one launch (start us, length us, event | category | flops | bytes accessed | tf_op | source)
XLA Modules:
  0.0 71.4 jit_solution(143908889825199303)
XLA Ops:
  0.7 0.0 copy-start.2
  0.7 0.0 copy-start.4
  0.7 1.0 %copy-done.2 = bf16[4,1,32,2240]{3,2,1,0:T(8,128)(2,1)S(1)} copy-done((bf16[4,1,32,2240]{3,2,1,0:T(8,128)(2,1)S(1)}, bf16[4,1,32,2240]{3,2,1,0:T(8,128)(2,1)}, u32[]{:S(2)}) %copy-start.2) | copy-done | bytes 573464
  1.7 0.2 turn.1.turned
  1.9 0.0 copy-done.4
  1.9 0.3 sent_states.1
  2.3 0.1 collective-permute-start
  2.4 0.4 kept_states.1
  2.7 1.1 %collective-permute-done = bf16[1024,128]{1,0:T(8,128)(2,1)S(1)} collective-permute-done((bf16[1024,128]{1,0:T(8,128)(2,1)S(1)}, bf16[1024,128]{1,0:T(8,128)(2,1)S(1)}, u32[]{:S(2)}, u32[]{:S(2)}) %collective-permute-start) | collective-permute-done | bytes 262176 | tf_op jit(solution)/shard_map/ppermute | solution.py:538
  3.9 0.1 add_convert_fusion
  3.9 24.5 %all_to_all.19.got_ref = bf16[32,32,128]{2,1,0:T(8,128)(2,1)S(1)} all-to-all(bf16[32,32,128]{2,1,0:T(8,128)(2,1)S(1)} %bitcast.23), channel_id=1, replica_groups=mesh['x'=4,'z'=8,'y'=4,'core'=2] {'z','y'}, dimensions={0} | all-to-all | bytes 524288 | tf_op jit(solution)/shard_map/all_to_all | solution.py:542
  28.5 9.1 %all_to_all.20.whole_ref = f32[4,32,128]{2,1,0:T(8,128)S(1)} all-to-all(f32[4,32,128]{2,1,0:T(8,128)S(1)} %get-tuple-element.13), channel_id=1, replica_groups=mesh['x'=4,'z'=8,'y'=4,'core'=2] {'x'}, dimensions={0} | all-to-all | bytes 131072 | tf_op jit(solution)/shard_map/all_to_all | solution.py:544
  37.6 15.7 %all_to_all.21 = bf16[32,32,128]{2,1,0:T(8,128)(2,1)S(1)} all-to-all(bf16[32,32,128]{2,1,0:T(8,128)(2,1)S(1)} %totals.1), channel_id=1, replica_groups=mesh['x'=4,'z'=8,'y'=4,'core'=2] {'z','y'}, dimensions={0} | all-to-all | bytes 524288 | tf_op jit(solution)/shard_map/all_to_all | solution.py:545
  53.4 0.0 collective-permute-start.1
  53.4 0.0 copy-done.5
  53.4 0.0 copy-done.1
  53.4 0.4 tail_own.1.own_attended
  53.8 1.1 %collective-permute-done.1.other_ref = bf16[1024,128]{1,0:T(8,128)(2,1)S(1)} collective-permute-done((bf16[1024,128]{1,0:T(8,128)(2,1)S(1)}, bf16[1024,128]{1,0:T(8,128)(2,1)S(1)}, u32[]{:S(2)}, u32[]{:S(2)}) %collective-permute-start.1) | collective-permute-done | bytes 262176 | tf_op jit(solution)/shard_map/ppermute | solution.py:547
  54.9 0.0 slice-done
  54.9 0.0 slice-done.1
  54.9 0.0 slice-done.2
  54.9 0.0 copy-done
  54.9 0.0 copy-start.3
  54.9 1.6 %tail_a.1 = (bf16[64,2240]{1,0:T(8,128)(2,1)S(1)}, bf16[64,1408]{1,0:T(8,128)(2,1)S(1)}) custom-call(s32[1]{0:T(128)S(6)} %copy.12.valid_ref, bf16[1024,128]{1,0:T(8,128)(2,1)S(1)} %collective-permute-done.1.other_ref, bf16[128,2240]{1,0:T(8,128)(2,1)S(1)} %bitcast.15, bf16[128,2240]{1,0:T(8,128)(2,1)S(1)} %bitcast.11, bf16[2240,2240]{1,0:T(8,128)(2,1)S(1)} %bitcast.10, ...), custom_call_target="tpu_custom_call" | custom-call | flops 3000000000 | bytes 1048576 | tf_op jit(solution)/shard_map/tail_a/pallas_call | solution.py:402
  56.5 0.8 %tail_b.1.right_ref = bf16[64,832]{1,0:T(8,128)(2,1)S(1)} custom-call(bf16[64,2240]{1,0:T(8,128)(2,1)S(1)} %get-tuple-element.15.attended, bf16[128,2240]{1,0:T(8,128)(2,1)S(1)} %bitcast.12, bf16[2240,2240]{1,0:T(8,128)(2,1)S(1)} %bitcast.10), custom_call_target="tpu_custom_call" | custom-call | flops 1000000000 | bytes 1048576 | tf_op jit(solution)/shard_map/tail_b/pallas_call | solution.py:423
  57.3 2.7 %collective-permute-start.3 = (bf16[64,832]{1,0:T(8,128)(2,1)S(1)}, bf16[64,832]{1,0:T(8,128)(2,1)S(1)}, u32[]{:S(2)}, u32[]{:S(2)}) collective-permute-start(bf16[64,832]{1,0:T(8,128)(2,1)S(1)} %tail_b.1.right_ref), channel_id=1, source_target_pairs={{0,8},{8,16},{16,24},{24,32},{32,40},{40,48},{48,56},{56,64},{64,7... | collective-permute-start | bytes 319496 | tf_op jit(solution)/shard_map/ppermute | solution.py:555
  60.0 2.5 %collective-permute-start.2 = (bf16[64,1408]{1,0:T(8,128)(2,1)S(1)}, bf16[64,1408]{1,0:T(8,128)(2,1)S(1)}, u32[]{:S(2)}, u32[]{:S(2)}) collective-permute-start(bf16[64,1408]{1,0:T(8,128)(2,1)S(1)} %get-tuple-element.14.left_ref), channel_id=1, source_target_pairs={{0,8},{8,16},{16,24},{24,32},{32,40},{40,48},{48,56},{56,64},{64,7... | collective-permute-start | bytes 540680 | tf_op jit(solution)/shard_map/ppermute | solution.py:553
  62.5 0.0 copy-done.3
  62.5 3.3 %head_of.1 = (bf16[128,2240]{1,0:T(8,128)(2,1)}, bf16[64,2240]{1,0:T(8,128)(2,1)S(1)}, f32[64,2240]{1,0:T(8,128)S(1)}) custom-call(s32[1]{0:T(128)S(6)} %copy.12.valid_ref, bf16[1024,128]{1,0:T(8,128)(2,1)S(1)} %bitcast.19, bf16[1024,128]{1,0:T(8,128)(2,1)S(1)} %collective-permute-done.1.other_ref, bf16[128,2240]{1,0:T(8,128)(2,1)S(1)} %bitcast.16, ...), custom_call_target="tpu_custom_call" | custom-call | flops 3000000000 | bytes 1048576 | tf_op jit(solution)/shard_map/head_of/pallas_call | solution.py:475
  65.7 0.8 %collective-permute-done.3.right_ref = bf16[64,832]{1,0:T(8,128)(2,1)S(1)} collective-permute-done((bf16[64,832]{1,0:T(8,128)(2,1)S(1)}, bf16[64,832]{1,0:T(8,128)(2,1)S(1)}, u32[]{:S(2)}, u32[]{:S(2)}) %collective-permute-start.3) | collective-permute-done | bytes 106528 | tf_op jit(solution)/shard_map/ppermute | solution.py:555
  66.5 3.8 %collective-permute-done.2.left_ref = bf16[64,1408]{1,0:T(8,128)(2,1)S(1)} collective-permute-done((bf16[64,1408]{1,0:T(8,128)(2,1)S(1)}, bf16[64,1408]{1,0:T(8,128)(2,1)S(1)}, u32[]{:S(2)}, u32[]{:S(2)}) %collective-permute-start.2) | collective-permute-done | bytes 180256 | tf_op jit(solution)/shard_map/ppermute | solution.py:553
  70.3 1.1 %finish.1 = bf16[128,2240]{1,0:T(8,128)(2,1)} custom-call(bf16[128,2240]{1,0:T(8,128)(2,1)} %get-tuple-element.16.unused_ref, bf16[64,2240]{1,0:T(8,128)(2,1)S(1)} %get-tuple-element.17.residual_ref, f32[64,2240]{1,0:T(8,128)S(1)} %get-tuple-element.18.partial_ref, ...), custom_call_target="tpu_custom_call", output_to_operand_aliasing={{}: (0, {})} | custom-call | flops 1000000000 | bytes 1048576 | tf_op jit(solution)/shard_map/finish/pallas_call | solution.py:516
  (11 shorter events, 0.1 us)
Async XLA Ops:
  0.7 1.1 %copy-start.2 = (bf16[4,1,32,2240]{3,2,1,0:T(8,128)(2,1)S(1)}, bf16[4,1,32,2240]{3,2,1,0:T(8,128)(2,1)}, u32[]{:S(2)}) copy-start(bf16[4,1,32,2240]{3,2,1,0:T(8,128)(2,1)} %param.9) | copy-start | bytes 1720324
  0.7 1.3 %copy-start.4 = (bf16[4,1,32,2240]{3,2,1,0:T(8,128)(2,1)S(1)}, bf16[4,1,32,2240]{3,2,1,0:T(8,128)(2,1)}, u32[]{:S(2)}) copy-start(bf16[4,1,32,2240]{3,2,1,0:T(8,128)(2,1)} %param.10) | copy-start | bytes 1720324
  2.3 1.6 %collective-permute-start = (bf16[1024,128]{1,0:T(8,128)(2,1)S(1)}, bf16[1024,128]{1,0:T(8,128)(2,1)S(1)}, u32[]{:S(2)}, u32[]{:S(2)}) collective-permute-start(bf16[1024,128]{1,0:T(8,128)(2,1)S(1)} %sent_states.1), channel_id=1, source_target_pairs={{0,1},{1,0},{2,3},{3,2},{4,5},{5,4},{6,7},{7,6},{8,9},{9,8},{10,11... | collective-permute-start | bytes 786440 | tf_op jit(solution)/shard_map/ppermute | solution.py:538
  28.5 26.4 %slice-start = ((s8[10321920]{0:T(1024)(128)(4,1)}), s8[4194304]{0:T(1024)(128)(4,1)S(1)}, s32[]{:S(2)}) async-start(s8[10321920]{0:T(1024)(128)(4,1)} %bitcast.9), calls=%async_computation.3 | async-start | bytes 8388608
  28.5 26.4 %slice-start.1 = ((s8[10321920]{0:T(1024)(128)(4,1)}), s8[4194304]{0:T(1024)(128)(4,1)S(1)}, s32[]{:S(2)}) async-start(s8[10321920]{0:T(1024)(128)(4,1)} %bitcast.9), calls=%async_computation.4 | async-start | bytes 8388608
  37.6 15.8 %copy-start.5 = (f32[2240]{0:T(1024)S(1)}, f32[2240]{0:T(1024)}, u32[]{:S(2)}) copy-start(f32[2240]{0:T(1024)} %param.13) | copy-start | bytes 26884
  37.6 15.8 %copy-start.1 = (bf16[4,1,32,2240]{3,2,1,0:T(8,128)(2,1)S(1)}, bf16[4,1,32,2240]{3,2,1,0:T(8,128)(2,1)}, u32[]{:S(2)}) copy-start(bf16[4,1,32,2240]{3,2,1,0:T(8,128)(2,1)} %param.8) | copy-start | bytes 1720324
  37.6 17.3 %slice-start.2 = ((s8[10321920]{0:T(1024)(128)(4,1)}), s8[1933312]{0:T(1024)(128)(4,1)S(1)}, s32[]{:S(2)}) async-start(s8[10321920]{0:T(1024)(128)(4,1)} %bitcast.9), calls=%async_computation.5 | async-start | bytes 3866624
  37.6 17.3 %copy-start = (bf16[4,1,32,2240]{3,2,1,0:T(8,128)(2,1)S(1)}, bf16[4,1,32,2240]{3,2,1,0:T(8,128)(2,1)}, u32[]{:S(2)}) copy-start(bf16[4,1,32,2240]{3,2,1,0:T(8,128)(2,1)} %param.11) | copy-start | bytes 1720324
  53.4 1.5 %collective-permute-start.1 = (bf16[1024,128]{1,0:T(8,128)(2,1)S(1)}, bf16[1024,128]{1,0:T(8,128)(2,1)S(1)}, u32[]{:S(2)}, u32[]{:S(2)}) collective-permute-start(bf16[1024,128]{1,0:T(8,128)(2,1)S(1)} %bitcast.17), channel_id=1, source_target_pairs={{0,1},{1,0},{2,3},{3,2},{4,5},{5,4},{6,7},{7,6},{8,9},{9,8},{10,11... | collective-permute-start | bytes 786440 | tf_op jit(solution)/shard_map/ppermute | solution.py:547
  54.9 7.5 %copy-start.3 = (f32[3,2240]{1,0:T(4,128)S(1)}, f32[3,2240]{1,0:T(4,128)}, u32[]{:S(2)}) copy-start(f32[3,2240]{1,0:T(4,128)} %taps_ref.3) | copy-start | bytes 80644
  57.3 9.2 %collective-permute-start.3 = (bf16[64,832]{1,0:T(8,128)(2,1)S(1)}, bf16[64,832]{1,0:T(8,128)(2,1)S(1)}, u32[]{:S(2)}, u32[]{:S(2)}) collective-permute-start(bf16[64,832]{1,0:T(8,128)(2,1)S(1)} %tail_b.1.right_ref), channel_id=1, source_target_pairs={{0,8},{8,16},{16,24},{24,32},{32,40},{40,48},{48,56},{56,64},{64,7... | collective-permute-start | bytes 319496 | tf_op jit(solution)/shard_map/ppermute | solution.py:555
  60.0 10.3 %collective-permute-start.2 = (bf16[64,1408]{1,0:T(8,128)(2,1)S(1)}, bf16[64,1408]{1,0:T(8,128)(2,1)S(1)}, u32[]{:S(2)}, u32[]{:S(2)}) collective-permute-start(bf16[64,1408]{1,0:T(8,128)(2,1)S(1)} %get-tuple-element.14.left_ref), channel_id=1, source_target_pairs={{0,8},{8,16},{16,24},{24,32},{32,40},{40,48},{48,56},{56,64},{64,7... | collective-permute-start | bytes 540680 | tf_op jit(solution)/shard_map/ppermute | solution.py:553

commit v4 on v3

--- a/solution.py
+++ b/solution.py
@@ -413,22 +413,27 @@
     )(valid, other, query, hidden, weight, own_attended)
 
 
-def tail_b_kernel(attended, hidden_ref, weight, residual):
+def tail_b_kernel(attended, hidden_ref, weight, left_ref, right_ref, residual):
     half, features = attended.shape
-    project_columns(attended, hidden_ref.at[half:, :], weight, residual, SPLIT, features)
-
-
-def tail_b(attended, hidden, weight):
+    project_columns(attended, hidden_ref.at[half:, :], weight, right_ref, SPLIT, features)
+    residual[:, :SPLIT] = left_ref[...]
+    residual[:, SPLIT:] = right_ref[...]
+
+
+def tail_b(attended, hidden, weight, left):
     half, features = attended.shape
     return pl.pallas_call(
         tail_b_kernel,
-        out_shape=jax.ShapeDtypeStruct((half, features - SPLIT), jnp.bfloat16),
-        in_specs=[vmem()] * 3,
-        out_specs=vmem(),
+        out_shape=(
+            jax.ShapeDtypeStruct((half, features - SPLIT), jnp.bfloat16),
+            jax.ShapeDtypeStruct((half, features), jnp.bfloat16),
+        ),
+        in_specs=[vmem()] * 4,
+        out_specs=(vmem(), vmem()),
         compiler_params=limit(24),
         cost_estimate=cost(1),
         name="tail_b",
-    )(attended, hidden, weight)
+    )(attended, hidden, weight, left)
 
 
 def head_kernel(
@@ -439,8 +444,7 @@
     hidden_ref,
     weight,
     gain_ref,
-    left_ref,
-    right_ref,
+    tail_ref,
     taps_ref,
     out_ref,
     residual,
@@ -451,7 +455,7 @@
     step = count // 2
     attend_rows(valid_ref, own_ref, other_ref, query_ref.at[:count, :], 0, attended)
     project_columns(attended, hidden_ref.at[:count, :], weight, residual, 0, features)
-    head, tail = (residual,), (left_ref, right_ref)
+    head, tail = (residual,), (tail_ref,)
     head_inverse, tail_inverse = inverse_of(head), inverse_of(tail)
     for s in range(0, features, LANES):
         w = min(LANES, features - s)
@@ -469,7 +473,7 @@
             out_ref[at, s : s + w] = (here[at] + temporal).astype(jnp.bfloat16)
 
 
-def head_of(valid, own, other, query, hidden, weight, gain, left, right, taps):
+def head_of(valid, own, other, query, hidden, weight, gain, tail, taps):
     tokens, features = query.shape
     half = (tokens // 2, features)
     return pl.pallas_call(
@@ -480,21 +484,24 @@
             jax.ShapeDtypeStruct(half, jnp.bfloat16),
             jax.ShapeDtypeStruct(half, jnp.float32),
         ),
-        in_specs=[smem()] + [vmem()] * 9,
+        in_specs=[smem()] + [vmem()] * 8,
         out_specs=(pl.BlockSpec(half, lambda i: (1, 0)), vmem(), vmem()),
         scratch_shapes=[pltpu.VMEM(half, jnp.bfloat16)],
         compiler_params=limit(24),
         cost_estimate=cost(3),
         name="head_of",
-    )(valid, own, other, query, hidden, weight, gain, left, right, taps)
+    )(valid, own, other, query, hidden, weight, gain, tail, taps)
 
 
 def finish_kernel(
-    unused_ref, residual_ref, partial_ref, left_ref, right_ref, gain_ref, taps_ref, out_ref
+    unused_ref, residual_ref, partial_ref, near_ref, left_ref, right_ref, gain_ref, taps_ref, out_ref, both
 ):
     count, features = residual_ref.shape
     step = count // 2
-    halo = (left_ref, right_ref)
+    edge = lax.axis_index("z") == 0
+    both[:, :SPLIT] = jnp.where(edge, left_ref[...], near_ref[:, :SPLIT])
+    both[:, SPLIT:] = jnp.where(edge, right_ref[...], near_ref[:, SPLIT:])
+    halo = (both,)
     inverse = inverse_of(halo)
     for s in range(0, features, LANES):
         w = min(LANES, features - s)
@@ -512,18 +519,19 @@
             out_ref[at, s : s + w] = (here + temporal).astype(jnp.bfloat16)
 
 
-def finish(out, residual, partial, left, right, gain, taps):
+def finish(out, residual, partial, near, left, right, gain, taps):
     return pl.pallas_call(
         finish_kernel,
         grid=(1,),
         out_shape=jax.ShapeDtypeStruct(out.shape, out.dtype),
-        in_specs=[pl.BlockSpec(memory_space=pl.ANY)] + [vmem()] * 6,
+        in_specs=[pl.BlockSpec(memory_space=pl.ANY)] + [vmem()] * 7,
         out_specs=pl.BlockSpec(residual.shape, lambda i: (0, 0)),
+        scratch_shapes=[pltpu.VMEM(residual.shape, jnp.bfloat16)],
         input_output_aliases={0: 0},
         compiler_params=limit(8),
         cost_estimate=cost(1),
         name="finish",
-    )(out, residual, partial, left, right, gain, taps)
+    )(out, residual, partial, near, left, right, gain, taps)
 
 
 def body(query_in, key_in, value_in, hidden_in, out_weight, norm_gain, temporal_taps, block_valid):
@@ -549,12 +557,15 @@
     gain = norm_gain.reshape(1, features)
     shared = (block_valid, own, other, query, hidden, out_weight)
     chain = [(i, i + 1) for i in range(X * Z - 1)]
+    within = [pair for pair in chain if pair[1] % Z]
+    across = [pair for pair in chain if pair[1] % Z == 0]
     attended, left = tail_a(block_valid, other, query, hidden, out_weight, own_attended)
-    halo_left = lax.ppermute(left, ("x", "z"), chain)
-    right = tail_b(attended, hidden, out_weight)
-    halo_right = lax.ppermute(right, ("x", "z"), chain)
-    out, residual, partial = head_of(*shared, gain, left, right, temporal_taps)
-    mixed = finish(out, residual, partial, halo_left, halo_right, gain, temporal_taps)
+    edge_left = lax.ppermute(left, ("x", "z"), across)
+    right, tail = tail_b(attended, hidden, out_weight, left)
+    edge_right = lax.ppermute(right, ("x", "z"), across)
+    near = lax.ppermute(tail, ("x", "z"), within)
+    out, residual, partial = head_of(*shared, gain, tail, temporal_taps)
+    mixed = finish(out, residual, partial, near, edge_left, edge_right, gain, temporal_taps)
     return mixed.reshape(query_in.shape)
 
 

time: 71.6 us -> 74.1 us (1.035)
  waiting for transfers between devices: 6.87 us -> 9.19 us
    ppermute x2 -> x3, waiting for transfers between devices: 4.6 us -> 6.89 us  [the longest x1 6.89 us: body(): edge_right = lax.ppermute(right, ('x', 'z'), across)]
    ppermute x2 -> x3, starting transfers between devices: 5.15 us -> 5.27 us  [the longest x1 2.68 us: body(): near = lax.ppermute(tail, ('x', 'z'), within)]
  transfers between devices with their start and end apart: 4 -> 5, of which waited for: 4 -> 3; matrix products, arithmetic and copies ran while one was open for 0% -> 0% of each run, Pallas kernels for 6% -> 5%
where the time goes in v4:
time: 74.1 us; the launch traced here: 73.9 us
  blocking collectives  49.3 us (67%)
  waiting for transfers between devices  9.19 us (12%)
  Pallas kernels  8.06 us (11%)
  starting transfers between devices  5.36 us (7%)
  local copies, waits for them, and re-layouts  1.07 us (1%)
  between operations  0.83 us (1%)
    all_to_all x1, blocking collectives, body(): lax.all_to_all(mine, ('z', 'y'), 0, 0, tiled=True)  24.5 us
    all_to_all x1, blocking collectives, body(): own = lax.all_to_all(totals(prefix, wholes), ('z', 'y'), 0, 0, tiled=True)  15.7 us
    all_to_all x1, blocking collectives, body(): wholes = lax.all_to_all(whole, 'x', 0, 0, tiled=True)  9.06 us
    ppermute x1, waiting for transfers between devices, body(): edge_right = lax.ppermute(right, ('x', 'z'), across)  6.89 us
    pallas_call x1, Pallas kernels, head_of(): pl.pallas_call(head_kernel, grid=(1,), out_shape=(jax.ShapeDtypeStruct(qu...  3.25 us
    ppermute x1, starting transfers between devices, body(): near = lax.ppermute(tail, ('x', 'z'), within)  2.68 us
    pallas_call x1, Pallas kernels, tail_a(): pl.pallas_call(tail_a_kernel, out_shape=(jax.ShapeDtypeStruct((tokens //...  1.57 us
  transfers between devices with their start and end apart: 5, of which 3 were waited for; matrix products, arithmetic and copies ran while one was open for 0% of the time, Pallas kernels for 5%

profile of v4, /device:TPU:2, one launch (start us, length us, event | category | flops | bytes accessed | tf_op | source)
XLA Modules:
  0.0 73.9 jit_solution(9499263693135650706)
XLA Ops:
  0.7 0.0 copy-start.2
  0.7 0.0 copy-start.4
  0.7 1.0 %copy-done.2 = bf16[4,1,32,2240]{3,2,1,0:T(8,128)(2,1)S(1)} copy-done((bf16[4,1,32,2240]{3,2,1,0:T(8,128)(2,1)S(1)}, bf16[4,1,32,2240]{3,2,1,0:T(8,128)(2,1)}, u32[]{:S(2)}) %copy-start.2) | copy-done | bytes 573464
  1.7 0.2 turn.1.turned
  1.9 0.0 copy-done.4
  1.9 0.3 sent_states.1
  2.3 0.1 collective-permute-start
  2.4 0.4 kept_states.1
  2.7 1.1 %collective-permute-done = bf16[1024,128]{1,0:T(8,128)(2,1)S(1)} collective-permute-done((bf16[1024,128]{1,0:T(8,128)(2,1)S(1)}, bf16[1024,128]{1,0:T(8,128)(2,1)S(1)}, u32[]{:S(2)}, u32[]{:S(2)}) %collective-permute-start) | collective-permute-done | bytes 262176 | tf_op jit(solution)/shard_map/ppermute | solution.py:546
  3.9 0.1 add_convert_fusion
  3.9 24.5 %all_to_all.19.got_ref = bf16[32,32,128]{2,1,0:T(8,128)(2,1)S(1)} all-to-all(bf16[32,32,128]{2,1,0:T(8,128)(2,1)S(1)} %bitcast.23), channel_id=1, replica_groups=mesh['x'=4,'z'=8,'y'=4,'core'=2] {'z','y'}, dimensions={0} | all-to-all | bytes 524288 | tf_op jit(solution)/shard_map/all_to_all | solution.py:550
  28.5 9.1 %all_to_all.20.whole_ref = f32[4,32,128]{2,1,0:T(8,128)S(1)} all-to-all(f32[4,32,128]{2,1,0:T(8,128)S(1)} %get-tuple-element.15), channel_id=1, replica_groups=mesh['x'=4,'z'=8,'y'=4,'core'=2] {'x'}, dimensions={0} | all-to-all | bytes 131072 | tf_op jit(solution)/shard_map/all_to_all | solution.py:552
  37.6 15.7 %all_to_all.21 = bf16[32,32,128]{2,1,0:T(8,128)(2,1)S(1)} all-to-all(bf16[32,32,128]{2,1,0:T(8,128)(2,1)S(1)} %totals.1), channel_id=1, replica_groups=mesh['x'=4,'z'=8,'y'=4,'core'=2] {'z','y'}, dimensions={0} | all-to-all | bytes 524288 | tf_op jit(solution)/shard_map/all_to_all | solution.py:553
  53.3 0.0 collective-permute-start.1
  53.4 0.0 copy-done.1
  53.4 0.4 tail_own.1.own_attended
  53.7 1.2 %collective-permute-done.1.other_ref = bf16[1024,128]{1,0:T(8,128)(2,1)S(1)} collective-permute-done((bf16[1024,128]{1,0:T(8,128)(2,1)S(1)}, bf16[1024,128]{1,0:T(8,128)(2,1)S(1)}, u32[]{:S(2)}, u32[]{:S(2)}) %collective-permute-start.1) | collective-permute-done | bytes 262176 | tf_op jit(solution)/shard_map/ppermute | solution.py:555
  54.9 0.0 slice-done
  54.9 0.0 slice-done.1
  54.9 0.0 copy-start.5
  54.9 0.0 copy-start.3
  54.9 1.6 %tail_a.1 = (bf16[64,2240]{1,0:T(8,128)(2,1)S(1)}, bf16[64,1408]{1,0:T(8,128)(2,1)S(1)}) custom-call(s32[1]{0:T(128)S(6)} %copy.12.valid_ref, bf16[1024,128]{1,0:T(8,128)(2,1)S(1)} %collective-permute-done.1.other_ref, bf16[128,2240]{1,0:T(8,128)(2,1)S(1)} %bitcast.15, bf16[128,2240]{1,0:T(8,128)(2,1)S(1)} %bitcast.11, bf16[2240,2240]{1,0:T(8,128)(2,1)S(1)} %bitcast.10, ...), custom_call_target="tpu_custom_call" | custom-call | flops 3000000000 | bytes 1048576 | tf_op jit(solution)/shard_map/tail_a/pallas_call | solution.py:402
  56.5 0.8 %tail_b.1 = (bf16[64,832]{1,0:T(8,128)(2,1)S(1)}, bf16[64,2240]{1,0:T(8,128)(2,1)S(1)}) custom-call(bf16[64,2240]{1,0:T(8,128)(2,1)S(1)} %get-tuple-element.16.attended, bf16[128,2240]{1,0:T(8,128)(2,1)S(1)} %bitcast.12, bf16[2240,2240]{1,0:T(8,128)(2,1)S(1)} %bitcast.10, bf16[64,1408]{1,0:T(8,128)(2,1)S(1)} %get-tuple-element.17.left_ref), custom_call_target="tpu_custom_call" | custom-call | flops 1000000000 | bytes 1048576 | tf_op jit(solution)/shard_map/tail_b/pallas_call | solution.py:425
  57.3 2.7 %collective-permute-start.2 = (bf16[64,2240]{1,0:T(8,128)(2,1)S(1)}, bf16[64,2240]{1,0:T(8,128)(2,1)S(1)}, u32[]{:S(2)}, u32[]{:S(2)}) collective-permute-start(bf16[64,2240]{1,0:T(8,128)(2,1)S(1)} %get-tuple-element.18.tail_ref), channel_id=1, source_target_pairs={{0,8},{8,16},{16,24},{24,32},{32,40},{40,48},{48,56},{64,72},{72,8... | collective-permute-start | bytes 860168 | tf_op jit(solution)/shard_map/ppermute | solution.py:566
  60.0 1.3 %collective-permute-start.3 = (bf16[64,1408]{1,0:T(8,128)(2,1)S(1)}, bf16[64,1408]{1,0:T(8,128)(2,1)S(1)}, u32[]{:S(2)}, u32[]{:S(2)}) collective-permute-start(bf16[64,1408]{1,0:T(8,128)(2,1)S(1)} %get-tuple-element.17.left_ref), channel_id=1, source_target_pairs={{56,64},{120,128},{184,192},{57,65},{121,129},{185,193},{58,66},{1... | collective-permute-start | bytes 540680 | tf_op jit(solution)/shard_map/ppermute | solution.py:563
  61.3 1.3 %collective-permute-start.4 = (bf16[64,832]{1,0:T(8,128)(2,1)S(1)}, bf16[64,832]{1,0:T(8,128)(2,1)S(1)}, u32[]{:S(2)}, u32[]{:S(2)}) collective-permute-start(bf16[64,832]{1,0:T(8,128)(2,1)S(1)} %get-tuple-element.22), channel_id=1, source_target_pairs={{56,64},{120,128},{184,192},{57,65},{121,129},{185,193},{58,66},{1... | collective-permute-start | bytes 319496 | tf_op jit(solution)/shard_map/ppermute | solution.py:565
  62.6 0.0 copy-done.3
  62.6 3.3 %head_of.1 = (bf16[128,2240]{1,0:T(8,128)(2,1)}, bf16[64,2240]{1,0:T(8,128)(2,1)S(1)}, f32[64,2240]{1,0:T(8,128)S(1)}) custom-call(s32[1]{0:T(128)S(6)} %copy.12.valid_ref, bf16[1024,128]{1,0:T(8,128)(2,1)S(1)} %bitcast.19, bf16[1024,128]{1,0:T(8,128)(2,1)S(1)} %collective-permute-done.1.other_ref, bf16[128,2240]{1,0:T(8,128)(2,1)S(1)} %bitcast.16, ...), custom_call_target="tpu_custom_call" | custom-call | flops 3000000000 | bytes 1048576 | tf_op jit(solution)/shard_map/head_of/pallas_call | solution.py:479
  65.9 6.9 %collective-permute-done.4.right_ref = bf16[64,832]{1,0:T(8,128)(2,1)S(1)} collective-permute-done((bf16[64,832]{1,0:T(8,128)(2,1)S(1)}, bf16[64,832]{1,0:T(8,128)(2,1)S(1)}, u32[]{:S(2)}, u32[]{:S(2)}) %collective-permute-start.4) | collective-permute-done | bytes 106528 | tf_op jit(solution)/shard_map/ppermute | solution.py:565
  72.8 0.0 collective-permute-done.3.left_ref
  72.8 0.0 collective-permute-done.2.near_ref
  72.8 1.1 %finish.1 = bf16[128,2240]{1,0:T(8,128)(2,1)} custom-call(bf16[128,2240]{1,0:T(8,128)(2,1)} %get-tuple-element.19.unused_ref, bf16[64,2240]{1,0:T(8,128)(2,1)S(1)} %get-tuple-element.20.residual_ref, f32[64,2240]{1,0:T(8,128)S(1)} %get-tuple-element.21.partial_ref, ...), custom_call_target="tpu_custom_call", output_to_operand_aliasing={{}: (0, {})} | custom-call | flops 1000000000 | bytes 1048576 | tf_op jit(solution)/shard_map/finish/pallas_call | solution.py:523
  (13 shorter events, 0.1 us)
Async XLA Ops:
  0.7 1.1 %copy-start.2 = (bf16[4,1,32,2240]{3,2,1,0:T(8,128)(2,1)S(1)}, bf16[4,1,32,2240]{3,2,1,0:T(8,128)(2,1)}, u32[]{:S(2)}) copy-start(bf16[4,1,32,2240]{3,2,1,0:T(8,128)(2,1)} %param.9) | copy-start | bytes 1720324
  0.7 1.3 %copy-start.4 = (bf16[4,1,32,2240]{3,2,1,0:T(8,128)(2,1)S(1)}, bf16[4,1,32,2240]{3,2,1,0:T(8,128)(2,1)}, u32[]{:S(2)}) copy-start(bf16[4,1,32,2240]{3,2,1,0:T(8,128)(2,1)} %param.10) | copy-start | bytes 1720324
  2.3 1.6 %collective-permute-start = (bf16[1024,128]{1,0:T(8,128)(2,1)S(1)}, bf16[1024,128]{1,0:T(8,128)(2,1)S(1)}, u32[]{:S(2)}, u32[]{:S(2)}) collective-permute-start(bf16[1024,128]{1,0:T(8,128)(2,1)S(1)} %sent_states.1), channel_id=1, source_target_pairs={{0,1},{1,0},{2,3},{3,2},{4,5},{5,4},{6,7},{7,6},{8,9},{9,8},{10,11... | collective-permute-start | bytes 786440 | tf_op jit(solution)/shard_map/ppermute | solution.py:546
  28.5 26.4 %slice-start = ((s8[10321920]{0:T(1024)(128)(4,1)}), s8[4194304]{0:T(1024)(128)(4,1)S(1)}, s32[]{:S(2)}) async-start(s8[10321920]{0:T(1024)(128)(4,1)} %bitcast.9), calls=%async_computation.3 | async-start | bytes 8388608
  28.5 26.4 %slice-start.1 = ((s8[10321920]{0:T(1024)(128)(4,1)}), s8[4194304]{0:T(1024)(128)(4,1)S(1)}, s32[]{:S(2)}) async-start(s8[10321920]{0:T(1024)(128)(4,1)} %bitcast.9), calls=%async_computation.4 | async-start | bytes 8388608
  37.6 15.8 %copy-start.1 = (bf16[4,1,32,2240]{3,2,1,0:T(8,128)(2,1)S(1)}, bf16[4,1,32,2240]{3,2,1,0:T(8,128)(2,1)}, u32[]{:S(2)}) copy-start(bf16[4,1,32,2240]{3,2,1,0:T(8,128)(2,1)} %param.8) | copy-start | bytes 1720324
  37.6 17.3 %slice-start.2 = ((s8[10321920]{0:T(1024)(128)(4,1)}), s8[1933312]{0:T(1024)(128)(4,1)S(1)}, s32[]{:S(2)}) async-start(s8[10321920]{0:T(1024)(128)(4,1)} %bitcast.9), calls=%async_computation.5 | async-start | bytes 3866624
  37.6 17.3 %copy-start = (bf16[4,1,32,2240]{3,2,1,0:T(8,128)(2,1)S(1)}, bf16[4,1,32,2240]{3,2,1,0:T(8,128)(2,1)}, u32[]{:S(2)}) copy-start(bf16[4,1,32,2240]{3,2,1,0:T(8,128)(2,1)} %param.11) | copy-start | bytes 1720324
  53.3 1.5 %collective-permute-start.1 = (bf16[1024,128]{1,0:T(8,128)(2,1)S(1)}, bf16[1024,128]{1,0:T(8,128)(2,1)S(1)}, u32[]{:S(2)}, u32[]{:S(2)}) collective-permute-start(bf16[1024,128]{1,0:T(8,128)(2,1)S(1)} %bitcast.17), channel_id=1, source_target_pairs={{0,1},{1,0},{2,3},{3,2},{4,5},{5,4},{6,7},{7,6},{8,9},{9,8},{10,11... | collective-permute-start | bytes 786440 | tf_op jit(solution)/shard_map/ppermute | solution.py:555
  54.9 5.1 %copy-start.5 = (f32[2240]{0:T(1024)S(1)}, f32[2240]{0:T(1024)}, u32[]{:S(2)}) copy-start(f32[2240]{0:T(1024)} %param.13) | copy-start | bytes 26884
  54.9 7.7 %copy-start.3 = (f32[3,2240]{1,0:T(4,128)S(1)}, f32[3,2240]{1,0:T(4,128)}, u32[]{:S(2)}) copy-start(f32[3,2240]{1,0:T(4,128)} %taps_ref.3) | copy-start | bytes 80644
  57.3 15.5 %collective-permute-start.2 = (bf16[64,2240]{1,0:T(8,128)(2,1)S(1)}, bf16[64,2240]{1,0:T(8,128)(2,1)S(1)}, u32[]{:S(2)}, u32[]{:S(2)}) collective-permute-start(bf16[64,2240]{1,0:T(8,128)(2,1)S(1)} %get-tuple-element.18.tail_ref), channel_id=1, source_target_pairs={{0,8},{8,16},{16,24},{24,32},{32,40},{40,48},{48,56},{64,72},{72,8... | collective-permute-start | bytes 860168 | tf_op jit(solution)/shard_map/ppermute | solution.py:566
  60.0 12.8 %collective-permute-start.3 = (bf16[64,1408]{1,0:T(8,128)(2,1)S(1)}, bf16[64,1408]{1,0:T(8,128)(2,1)S(1)}, u32[]{:S(2)}, u32[]{:S(2)}) collective-permute-start(bf16[64,1408]{1,0:T(8,128)(2,1)S(1)} %get-tuple-element.17.left_ref), channel_id=1, source_target_pairs={{56,64},{120,128},{184,192},{57,65},{121,129},{185,193},{58,66},{1... | collective-permute-start | bytes 540680 | tf_op jit(solution)/shard_map/ppermute | solution.py:563
  61.3 11.5 %collective-permute-start.4 = (bf16[64,832]{1,0:T(8,128)(2,1)S(1)}, bf16[64,832]{1,0:T(8,128)(2,1)S(1)}, u32[]{:S(2)}, u32[]{:S(2)}) collective-permute-start(bf16[64,832]{1,0:T(8,128)(2,1)S(1)} %get-tuple-element.22), channel_id=1, source_target_pairs={{56,64},{120,128},{184,192},{57,65},{121,129},{185,193},{58,66},{1... | collective-permute-start | bytes 319496 | tf_op jit(solution)/shard_map/ppermute | solution.py:565

commit v5 on v3

--- a/solution.py
+++ b/solution.py
@@ -310,31 +310,9 @@
     if group:
         store_end(attended, carry)
     else:
-        tile = place_of(GROUP)[0] * LANES
-        attended[:, tile : tile + LANES] = carry.astype(jnp.bfloat16)
-
-
-def tail_own_kernel(valid_ref, own_ref, query_ref, attended):
-    half = query_ref.shape[0] // 2
-    core = lax.axis_index("core")
-    for group in range(2):
-
-        @pl.when(core == group)
-        def _():
-            attend_half(group, valid_ref, own_ref, query_ref.at[half:, :], attended)
-
-
-def tail_own(valid, own, query):
-    tokens, features = query.shape
-    return pl.pallas_call(
-        tail_own_kernel,
-        out_shape=jax.ShapeDtypeStruct((tokens // 2, features), jnp.bfloat16),
-        in_specs=[smem(), vmem(), vmem()],
-        out_specs=vmem(),
-        compiler_params=limit(8),
-        cost_estimate=cost(1),
-        name="tail_own",
-    )(valid, own, query)
+        tile, off = place_of(GROUP)
+        kept = jnp.where(lane_of((count, LANES)) < off, carry, 0.0)
+        attended[:, tile * LANES : (tile + 1) * LANES] = kept.astype(jnp.bfloat16)
 
 
 def project_columns(attended, hidden_ref, weight, residual, start, stop):
@@ -375,29 +353,70 @@
         s -= part.shape[1]
 
 
+def rows_of(group, features):
+    edge = place_of(GROUP)[0] * LANES
+    return slice(edge, features) if group else slice(0, edge + LANES)
+
+
+def partial_product(group, attended, weight, start, stop):
+    rows = rows_of(group, weight.shape[0])
+    return jnp.dot(
+        attended[:, rows], weight[rows, start:stop], preferred_element_type=jnp.float32
+    )
+
+
+def tail_own_kernel(valid_ref, own_ref, query_ref, weight, summed, attended):
+    count, features = summed.shape
+    core = lax.axis_index("core")
+    for group in range(2):
+
+        @pl.when(core == group)
+        def _():
+            attend_half(group, valid_ref, own_ref, query_ref.at[count:, :], attended)
+            for s in range(0, features, CHUNK):
+                e = min(s + CHUNK, features)
+                summed[:, s:e] = partial_product(group, attended, weight, s, e)
+
+
+def tail_own(valid, own, query, weight):
+    tokens, features = query.shape
+    half = (tokens // 2, features)
+    return pl.pallas_call(
+        tail_own_kernel,
+        out_shape=jax.ShapeDtypeStruct(half, jnp.float32),
+        in_specs=[smem(), vmem(), vmem(), vmem()],
+        out_specs=vmem(),
+        scratch_shapes=[pltpu.VMEM(half, jnp.bfloat16)],
+        compiler_params=limit(24),
+        cost_estimate=cost(1),
+        name="tail_own",
+    )(valid, own, query, weight)
+
+
+def add_columns(group, attended, summed, hidden_ref, weight, residual, start, stop):
+    for s in range(start, stop, CHUNK):
+        at = slice(s, min(s + CHUNK, stop))
+        projected = summed[:, at] + partial_product(group, attended, weight, at.start, at.stop)
+        rounded = (hidden_ref[:, at].astype(jnp.float32) + projected).astype(jnp.bfloat16)
+        residual[:, at.start - start : at.stop - start] = rounded
+
+
 def tail_a_kernel(
-    valid_ref, other_ref, query_ref, hidden_ref, weight, own_attended, attended, residual
+    valid_ref, other_ref, query_ref, hidden_ref, weight, summed, attended, residual
 ):
-    count, features = attended.shape
+    count = attended.shape[0]
     core = lax.axis_index("core")
-    tile, off = place_of(GROUP)
-    shared = slice(tile * LANES, (tile + 1) * LANES)
-    lane = lane_of((count, LANES))
     for group in range(2):
 
         @pl.when(core == 1 - group)
         def _():
             attend_half(group, valid_ref, other_ref, query_ref.at[count:, :], attended)
-            done = slice(shared.stop, features) if group == 0 else slice(0, shared.start)
-            attended[:, done] = own_attended[:, done]
-            first = (attended if group == 0 else own_attended)[:, shared]
-            second = (own_attended if group == 0 else attended)[:, shared]
-            attended[:, shared] = jnp.where(lane < off, first, second)
-
-    project_columns(attended, hidden_ref.at[count:, :], weight, residual, 0, SPLIT)
-
-
-def tail_a(valid, other, query, hidden, weight, own_attended):
+            add_columns(
+                group, attended, summed, hidden_ref.at[count:, :], weight, residual, 0, SPLIT
+            )
+
+
+def tail_a(valid, other, query, hidden, weight, summed):
     tokens, features = query.shape
     return pl.pallas_call(
         tail_a_kernel,
@@ -410,25 +429,32 @@
         compiler_params=limit(24),
         cost_estimate=cost(3),
         name="tail_a",
-    )(valid, other, query, hidden, weight, own_attended)
-
-
-def tail_b_kernel(attended, hidden_ref, weight, residual):
+    )(valid, other, query, hidden, weight, summed)
+
+
+def tail_b_kernel(attended, hidden_ref, weight, summed, residual):
     half, features = attended.shape
-    project_columns(attended, hidden_ref.at[half:, :], weight, residual, SPLIT, features)
-
-
-def tail_b(attended, hidden, weight):
+    core = lax.axis_index("core")
+    for group in range(2):
+
+        @pl.when(core == 1 - group)
+        def _():
+            add_columns(
+                group, attended, summed, hidden_ref.at[half:, :], weight, residual, SPLIT, features
+            )
+
+
+def tail_b(attended, hidden, weight, summed):
     half, features = attended.shape
     return pl.pallas_call(
         tail_b_kernel,
         out_shape=jax.ShapeDtypeStruct((half, features - SPLIT), jnp.bfloat16),
-        in_specs=[vmem()] * 3,
+        in_specs=[vmem()] * 4,
         out_specs=vmem(),
         compiler_params=limit(24),
         cost_estimate=cost(1),
         name="tail_b",
-    )(attended, hidden, weight)
+    )(attended, hidden, weight, summed)
 
 
 def head_kernel(
@@ -545,13 +571,13 @@
     own = lax.all_to_all(totals(prefix, wholes), ("z", "y"), 0, 0, tiled=True)
     own = own.reshape(ROWS, LANES)
     other = lax.ppermute(own, "core", swap)
-    own_attended = tail_own(block_valid, own, query)
+    summed = tail_own(block_valid, own, query, out_weight)
     gain = norm_gain.reshape(1, features)
     shared = (block_valid, own, other, query, hidden, out_weight)
     chain = [(i, i + 1) for i in range(X * Z - 1)]
-    attended, left = tail_a(block_valid, other, query, hidden, out_weight, own_attended)
+    attended, left = tail_a(block_valid, other, query, hidden, out_weight, summed)
     halo_left = lax.ppermute(left, ("x", "z"), chain)
-    right = tail_b(attended, hidden, out_weight)
+    right = tail_b(attended, hidden, out_weight, summed)
     halo_right = lax.ppermute(right, ("x", "z"), chain)
     out, residual, partial = head_of(*shared, gain, left, right, temporal_taps)
     mixed = finish(out, residual, partial, halo_left, halo_right, gain, temporal_taps)

time: 71.6 us -> 71 us (level)
    ppermute x1, waiting for transfers between devices: 1.12 us -> 0.12 us  [body(): other = lax.ppermute(own, 'core', swap)]
    pallas_call x1, Pallas kernels: 0.38 us -> 1.34 us  [tail_own(): pl.pallas_call(tail_own_kernel, out_shape=jax.ShapeDtypeStruct(half, jnp....]
  transfers between devices with their start and end apart: 4 -> 4, of which waited for: 4 -> 4; matrix products, arithmetic and copies ran while one was open for 0% -> 0% of each run, Pallas kernels for 6% -> 7%
where the time goes in v5:
time: 71 us; the launch traced here: 70.8 us
  blocking collectives  49.3 us (69%)
  Pallas kernels  8.12 us (11%)
  waiting for transfers between devices  6.19 us (9%)
  starting transfers between devices  5.24 us (7%)
  local copies, waits for them, and re-layouts  1.06 us (1%)
  between operations  0.83 us (1%)
    all_to_all x1, blocking collectives, body(): lax.all_to_all(mine, ('z', 'y'), 0, 0, tiled=True)  24.5 us
    all_to_all x1, blocking collectives, body(): own = lax.all_to_all(totals(prefix, wholes), ('z', 'y'), 0, 0, tiled=True)  15.7 us
    all_to_all x1, blocking collectives, body(): wholes = lax.all_to_all(whole, 'x', 0, 0, tiled=True)  9.06 us
    ppermute x1, waiting for transfers between devices, body(): halo_left = lax.ppermute(left, ('x', 'z'), chain)  3.8 us
    pallas_call x1, Pallas kernels, head_of(): pl.pallas_call(head_kernel, grid=(1,), out_shape=(jax.ShapeDtypeStruct(qu...  3.26 us
    ppermute x1, starting transfers between devices, body(): halo_right = lax.ppermute(right, ('x', 'z'), chain)  2.67 us
    ppermute x1, starting transfers between devices, body(): halo_left = lax.ppermute(left, ('x', 'z'), chain)  2.48 us
  transfers between devices with their start and end apart: 4, of which 4 were waited for; matrix products, arithmetic and copies ran while one was open for 0% of the time, Pallas kernels for 7%

profile of v5, /device:TPU:2, one launch (start us, length us, event | category | flops | bytes accessed | tf_op | source)
XLA Modules:
  0.0 70.8 jit_solution(1150337648681713997)
XLA Ops:
  0.7 0.0 copy-start.2
  0.7 0.0 copy-start.4
  0.7 1.0 %copy-done.2 = bf16[4,1,32,2240]{3,2,1,0:T(8,128)(2,1)S(1)} copy-done((bf16[4,1,32,2240]{3,2,1,0:T(8,128)(2,1)S(1)}, bf16[4,1,32,2240]{3,2,1,0:T(8,128)(2,1)}, u32[]{:S(2)}) %copy-start.2) | copy-done | bytes 573464
  1.7 0.2 turn.1.turned
  1.9 0.0 copy-done.4
  1.9 0.3 sent_states.1
  2.3 0.1 collective-permute-start
  2.4 0.4 kept_states.1
  2.7 1.1 %collective-permute-done = bf16[1024,128]{1,0:T(8,128)(2,1)S(1)} collective-permute-done((bf16[1024,128]{1,0:T(8,128)(2,1)S(1)}, bf16[1024,128]{1,0:T(8,128)(2,1)S(1)}, u32[]{:S(2)}, u32[]{:S(2)}) %collective-permute-start) | collective-permute-done | bytes 262176 | tf_op jit(solution)/shard_map/ppermute | solution.py:564
  3.9 0.1 add_convert_fusion
  3.9 24.5 %all_to_all.19.got_ref = bf16[32,32,128]{2,1,0:T(8,128)(2,1)S(1)} all-to-all(bf16[32,32,128]{2,1,0:T(8,128)(2,1)S(1)} %bitcast.23), channel_id=1, replica_groups=mesh['x'=4,'z'=8,'y'=4,'core'=2] {'z','y'}, dimensions={0} | all-to-all | bytes 524288 | tf_op jit(solution)/shard_map/all_to_all | solution.py:568
  28.5 9.1 %all_to_all.20.whole_ref = f32[4,32,128]{2,1,0:T(8,128)S(1)} all-to-all(f32[4,32,128]{2,1,0:T(8,128)S(1)} %get-tuple-element.13), channel_id=1, replica_groups=mesh['x'=4,'z'=8,'y'=4,'core'=2] {'x'}, dimensions={0} | all-to-all | bytes 131072 | tf_op jit(solution)/shard_map/all_to_all | solution.py:570
  37.6 0.0 copy-start.1
  37.6 15.7 %all_to_all.21 = bf16[32,32,128]{2,1,0:T(8,128)(2,1)S(1)} all-to-all(bf16[32,32,128]{2,1,0:T(8,128)(2,1)S(1)} %totals.1), channel_id=1, replica_groups=mesh['x'=4,'z'=8,'y'=4,'core'=2] {'z','y'}, dimensions={0} | all-to-all | bytes 524288 | tf_op jit(solution)/shard_map/all_to_all | solution.py:571
  53.4 0.0 collective-permute-start.1
  53.4 0.0 copy-done.5
  53.4 0.0 slice-done
  53.4 0.0 slice-done.1
  53.4 0.0 slice-done.2
  53.4 0.0 copy-done
  53.4 1.3 %tail_own.1.summed = f32[64,2240]{1,0:T(8,128)S(1)} custom-call(s32[1]{0:T(128)S(6)} %copy.12.valid_ref, bf16[1024,128]{1,0:T(8,128)(2,1)S(1)} %bitcast.18, bf16[128,2240]{1,0:T(8,128)(2,1)S(1)} %bitcast.11, bf16[2240,2240]{1,0:T(8,128)(2,1)S(1)} %bitcast.10), custom_call_target="tpu_custom_call" | custom-call | flops 1000000000 | bytes 1048576 | tf_op jit(solution)/shard_map/tail_own/pallas_call | solution.py:384
  54.8 0.1 collective-permute-done.1.other_ref
  54.9 0.0 copy-done.1
  54.9 1.0 %tail_a.1 = (bf16[64,2240]{1,0:T(8,128)(2,1)S(1)}, bf16[64,1408]{1,0:T(8,128)(2,1)S(1)}) custom-call(s32[1]{0:T(128)S(6)} %copy.12.valid_ref, bf16[1024,128]{1,0:T(8,128)(2,1)S(1)} %collective-permute-done.1.other_ref, bf16[128,2240]{1,0:T(8,128)(2,1)S(1)} %bitcast.12, bf16[128,2240]{1,0:T(8,128)(2,1)S(1)} %bitcast.14, bf16[2240,2240]{1,0:T(8,128)(2,1)S(1)} %bitcast.10, ...), custom_call_target="tpu_custom_call" | custom-call | flops 3000000000 | bytes 1048576 | tf_op jit(solution)/shard_map/tail_a/pallas_call | solution.py:421
  55.9 0.5 tail_b.1.right_ref
  56.4 2.7 %collective-permute-start.3 = (bf16[64,832]{1,0:T(8,128)(2,1)S(1)}, bf16[64,832]{1,0:T(8,128)(2,1)S(1)}, u32[]{:S(2)}, u32[]{:S(2)}) collective-permute-start(bf16[64,832]{1,0:T(8,128)(2,1)S(1)} %tail_b.1.right_ref), channel_id=1, source_target_pairs={{0,8},{8,16},{16,24},{24,32},{32,40},{40,48},{48,56},{56,64},{64,7... | collective-permute-start | bytes 319496 | tf_op jit(solution)/shard_map/ppermute | solution.py:581
  59.1 2.5 %collective-permute-start.2 = (bf16[64,1408]{1,0:T(8,128)(2,1)S(1)}, bf16[64,1408]{1,0:T(8,128)(2,1)S(1)}, u32[]{:S(2)}, u32[]{:S(2)}) collective-permute-start(bf16[64,1408]{1,0:T(8,128)(2,1)S(1)} %get-tuple-element.14.left_ref), channel_id=1, source_target_pairs={{0,8},{8,16},{16,24},{24,32},{32,40},{40,48},{48,56},{56,64},{64,7... | collective-permute-start | bytes 540680 | tf_op jit(solution)/shard_map/ppermute | solution.py:579
  61.6 0.0 copy-done.3
  61.6 3.3 %head_of.1 = (bf16[128,2240]{1,0:T(8,128)(2,1)}, bf16[64,2240]{1,0:T(8,128)(2,1)S(1)}, f32[64,2240]{1,0:T(8,128)S(1)}) custom-call(s32[1]{0:T(128)S(6)} %copy.12.valid_ref, bf16[1024,128]{1,0:T(8,128)(2,1)S(1)} %bitcast.19, bf16[1024,128]{1,0:T(8,128)(2,1)S(1)} %collective-permute-done.1.other_ref, bf16[128,2240]{1,0:T(8,128)(2,1)S(1)} %bitcast.13, ...), custom_call_target="tpu_custom_call" | custom-call | flops 3000000000 | bytes 1048576 | tf_op jit(solution)/shard_map/head_of/pallas_call | solution.py:501
  64.8 1.1 %collective-permute-done.3.right_ref = bf16[64,832]{1,0:T(8,128)(2,1)S(1)} collective-permute-done((bf16[64,832]{1,0:T(8,128)(2,1)S(1)}, bf16[64,832]{1,0:T(8,128)(2,1)S(1)}, u32[]{:S(2)}, u32[]{:S(2)}) %collective-permute-start.3) | collective-permute-done | bytes 106528 | tf_op jit(solution)/shard_map/ppermute | solution.py:581
  65.9 3.8 %collective-permute-done.2.left_ref = bf16[64,1408]{1,0:T(8,128)(2,1)S(1)} collective-permute-done((bf16[64,1408]{1,0:T(8,128)(2,1)S(1)}, bf16[64,1408]{1,0:T(8,128)(2,1)S(1)}, u32[]{:S(2)}, u32[]{:S(2)}) %collective-permute-start.2) | collective-permute-done | bytes 180256 | tf_op jit(solution)/shard_map/ppermute | solution.py:579
  69.7 1.1 %finish.1 = bf16[128,2240]{1,0:T(8,128)(2,1)} custom-call(bf16[128,2240]{1,0:T(8,128)(2,1)} %get-tuple-element.16.unused_ref, bf16[64,2240]{1,0:T(8,128)(2,1)S(1)} %get-tuple-element.17.residual_ref, f32[64,2240]{1,0:T(8,128)S(1)} %get-tuple-element.18.partial_ref, ...), custom_call_target="tpu_custom_call", output_to_operand_aliasing={{}: (0, {})} | custom-call | flops 1000000000 | bytes 1048576 | tf_op jit(solution)/shard_map/finish/pallas_call | solution.py:542
  (11 shorter events, 0.1 us)
Async XLA Ops:
  0.7 1.1 %copy-start.2 = (bf16[4,1,32,2240]{3,2,1,0:T(8,128)(2,1)S(1)}, bf16[4,1,32,2240]{3,2,1,0:T(8,128)(2,1)}, u32[]{:S(2)}) copy-start(bf16[4,1,32,2240]{3,2,1,0:T(8,128)(2,1)} %param.9) | copy-start | bytes 1720324
  0.7 1.3 %copy-start.4 = (bf16[4,1,32,2240]{3,2,1,0:T(8,128)(2,1)S(1)}, bf16[4,1,32,2240]{3,2,1,0:T(8,128)(2,1)}, u32[]{:S(2)}) copy-start(bf16[4,1,32,2240]{3,2,1,0:T(8,128)(2,1)} %param.10) | copy-start | bytes 1720324
  2.3 1.6 %collective-permute-start = (bf16[1024,128]{1,0:T(8,128)(2,1)S(1)}, bf16[1024,128]{1,0:T(8,128)(2,1)S(1)}, u32[]{:S(2)}, u32[]{:S(2)}) collective-permute-start(bf16[1024,128]{1,0:T(8,128)(2,1)S(1)} %sent_states.1), channel_id=1, source_target_pairs={{0,1},{1,0},{2,3},{3,2},{4,5},{5,4},{6,7},{7,6},{8,9},{9,8},{10,11... | collective-permute-start | bytes 786440 | tf_op jit(solution)/shard_map/ppermute | solution.py:564
  28.5 24.9 %slice-start = ((s8[10321920]{0:T(1024)(128)(4,1)}), s8[4194304]{0:T(1024)(128)(4,1)S(1)}, s32[]{:S(2)}) async-start(s8[10321920]{0:T(1024)(128)(4,1)} %bitcast.9), calls=%async_computation.3 | async-start | bytes 8388608
  28.5 24.9 %slice-start.1 = ((s8[10321920]{0:T(1024)(128)(4,1)}), s8[4194304]{0:T(1024)(128)(4,1)S(1)}, s32[]{:S(2)}) async-start(s8[10321920]{0:T(1024)(128)(4,1)} %bitcast.9), calls=%async_computation.4 | async-start | bytes 8388608
  37.6 15.8 %copy-start.5 = (f32[2240]{0:T(1024)S(1)}, f32[2240]{0:T(1024)}, u32[]{:S(2)}) copy-start(f32[2240]{0:T(1024)} %param.13) | copy-start | bytes 26884
  37.6 15.8 %slice-start.2 = ((s8[10321920]{0:T(1024)(128)(4,1)}), s8[1933312]{0:T(1024)(128)(4,1)S(1)}, s32[]{:S(2)}) async-start(s8[10321920]{0:T(1024)(128)(4,1)} %bitcast.9), calls=%async_computation.5 | async-start | bytes 3866624
  37.6 15.8 %copy-start = (bf16[4,1,32,2240]{3,2,1,0:T(8,128)(2,1)S(1)}, bf16[4,1,32,2240]{3,2,1,0:T(8,128)(2,1)}, u32[]{:S(2)}) copy-start(bf16[4,1,32,2240]{3,2,1,0:T(8,128)(2,1)} %param.8) | copy-start | bytes 1720324
  37.6 17.3 %copy-start.1 = (bf16[4,1,32,2240]{3,2,1,0:T(8,128)(2,1)S(1)}, bf16[4,1,32,2240]{3,2,1,0:T(8,128)(2,1)}, u32[]{:S(2)}) copy-start(bf16[4,1,32,2240]{3,2,1,0:T(8,128)(2,1)} %param.11) | copy-start | bytes 1720324
  53.4 1.5 %collective-permute-start.1 = (bf16[1024,128]{1,0:T(8,128)(2,1)S(1)}, bf16[1024,128]{1,0:T(8,128)(2,1)S(1)}, u32[]{:S(2)}, u32[]{:S(2)}) collective-permute-start(bf16[1024,128]{1,0:T(8,128)(2,1)S(1)} %bitcast.17), channel_id=1, source_target_pairs={{0,1},{1,0},{2,3},{3,2},{4,5},{5,4},{6,7},{7,6},{8,9},{9,8},{10,11... | collective-permute-start | bytes 786440 | tf_op jit(solution)/shard_map/ppermute | solution.py:573
  54.9 6.7 %copy-start.3 = (f32[3,2240]{1,0:T(4,128)S(1)}, f32[3,2240]{1,0:T(4,128)}, u32[]{:S(2)}) copy-start(f32[3,2240]{1,0:T(4,128)} %taps_ref.3) | copy-start | bytes 80644
  56.4 9.6 %collective-permute-start.3 = (bf16[64,832]{1,0:T(8,128)(2,1)S(1)}, bf16[64,832]{1,0:T(8,128)(2,1)S(1)}, u32[]{:S(2)}, u32[]{:S(2)}) collective-permute-start(bf16[64,832]{1,0:T(8,128)(2,1)S(1)} %tail_b.1.right_ref), channel_id=1, source_target_pairs={{0,8},{8,16},{16,24},{24,32},{32,40},{40,48},{48,56},{56,64},{64,7... | collective-permute-start | bytes 319496 | tf_op jit(solution)/shard_map/ppermute | solution.py:581
  59.1 10.7 %collective-permute-start.2 = (bf16[64,1408]{1,0:T(8,128)(2,1)S(1)}, bf16[64,1408]{1,0:T(8,128)(2,1)S(1)}, u32[]{:S(2)}, u32[]{:S(2)}) collective-permute-start(bf16[64,1408]{1,0:T(8,128)(2,1)S(1)} %get-tuple-element.14.left_ref), channel_id=1, source_target_pairs={{0,8},{8,16},{16,24},{24,32},{32,40},{40,48},{48,56},{56,64},{64,7... | collective-permute-start | bytes 540680 | tf_op jit(solution)/shard_map/ppermute | solution.py:579
